TPU v7x, 128 devices: a whole 4x4x4 slice. The times are simulated.
128 devices in a mesh: wrap: 16 (over y_lo, z, core), span: 8 (over x, y_hi).
Axes of the slice: x: 4, y: 4 (y_hi: 2, y_lo: 2; y = y_hi * 2 + y_lo), z: 4, core: 2. Of those that a mesh axis runs over, the one named last changes fastest.
Arguments:
- adjoint_start: float32 [5, 32, 256, 1024], P(None, None, 'wrap', 'span'), may hold values from -6 to 6
- adjoint_source: float32 [5, 32, 256, 1024], P(None, None, 'wrap', 'span'), may hold values from -6 to 6
- jacobians: bfloat16 [3, 5, 5, 32, 256, 1024], P(None, None, None, None, 'wrap', 'span'), may hold values from -1.1953125 to 1.1953125
- dissipation: float32 [32, 256, 1024], P(None, 'wrap', 'span'), may hold values from 0.5 to 2
- wall_mask: int32 [256, 1024], P('wrap', 'span'), may hold values from 0 to 1, as said below
- wake_partner: int32 [256, 1024], P('wrap', 'span'), may hold values from 0 to 255, as said below
- surface_slopes: float32 [3, 5, 256, 1024], P(None, None, 'wrap', 'span'), may hold values from -2.5 to 2.5
- control_points: int32 [4, 256, 1024], P(None, 'wrap', 'span'), may hold values from 0 to 1023
- control_weights: float32 [4, 256, 1024], P(None, 'wrap', 'span'), may hold values from 0.02 to 0.1
Outputs:
- adjoint_final: float32 [5, 32, 256, 1024], P(None, None, 'wrap', 'span')
- residual: float32 [5, 32, 256, 1024], P(None, None, 'wrap', 'span')
- shape_gradient: float32 [3, 1024], P(None, ('wrap', 'span'))
Inputs may be any that keep to these rules, and one draw needn't show every extreme that they name: `wall_mask`: 1 marks wall, 0 the wake cut; the wall covers one middle range of the wrap index and the span indices below a tip index; both kinds occur. wake_partner[i, k] lies within 1 of 255 - i, and equals it at i = 0 and i = 255.
All inputs are finite; a program needn't handle non-finite values.
Results may differ from a plain program's by a relative error of at most 0.0003.
Values sent between devices are 32-bit elements; how exact they have to be, the bound alone decides.
No kernel may reach another device: no remote copies, remote signals or barrier semaphores. Data moves between devices by JAX's collectives and lax.ppermute only.
A program may use at most 128 MiB of HBM per device.

v0:
```python
import functools

import jax
import jax.numpy as jnp
from jax import lax
from jax.experimental import pallas as pl
from jax.experimental.pallas import tpu as pltpu
from jax.sharding import PartitionSpec as P

COMPS = 5
NJ = 32
ROWS = 16
LANES = 128
HALF = 8
WRAP = 16
SPAN = 8
LISTS = 4
OMEGA = 0.8
F32 = jnp.float32
BF16 = jnp.bfloat16
VSPEC = pl.BlockSpec(memory_space=pltpu.VMEM)


def shape_of(*dims, dtype=F32):
    return jax.ShapeDtypeStruct(dims, dtype)


FARSPEC = pl.BlockSpec(memory_space=pltpu.HBM)


def run_kernel(
    kernel,
    outs,
    args,
    scratch=(),
    aliases=None,
    flops=0,
    name=None,
    far=(),
    far_out=(),
    vmem=4,
):
    moved = sum(a.size * a.dtype.itemsize for a in args)
    return pl.pallas_call(
        kernel,
        out_shape=outs,
        in_specs=[FARSPEC if n in far else VSPEC for n in range(len(args))],
        out_specs=[FARSPEC if n in far_out else VSPEC for n in range(len(outs))],
        scratch_shapes=list(scratch),
        input_output_aliases=aliases or {},
        compiler_params=pltpu.CompilerParams(vmem_limit_bytes=int(vmem * 2**20)),
        cost_estimate=pl.CostEstimate(flops=flops, transcendentals=0, bytes_accessed=moved),
        name=name,
    )(*args)


def lane_index():
    return lax.broadcasted_iota(jnp.int32, (HALF, LANES), 1)


def row_index():
    return lax.broadcasted_iota(jnp.int32, (HALF, LANES), 0)


def spread(row):
    return jnp.broadcast_to(row, (HALF, LANES))


def pack_edges(packed, halves, j, lane):
    for half in range(2):
        m = 2 * j + half
        here = (lane >> 1) == m
        for c in range(COMPS):
            packed[c] = jnp.where(here, pltpu.roll(halves[c][half], 2 * m + 1, 1), packed[c])
    return packed


def first_faces(start_ref, v_ref, slab_ref, low_ref, high_ref, edge_ref, sem):
    lane = lane_index()
    copy = pltpu.make_async_copy(start_ref, v_ref.at[:, :NJ], sem)
    copy.start()
    for c in range(COMPS):
        v_ref[c, NJ] = jnp.zeros((ROWS, LANES), F32)
    copy.wait()

    def step(j, packed):
        halves = [(v_ref[c, j, :HALF], v_ref[c, j, HALF:]) for c in range(COMPS)]
        for c in range(COMPS):
            low_ref[c, pl.ds(j, 1)] = halves[c][0][:1]
            high_ref[c, pl.ds(j, 1)] = halves[c][1][HALF - 1 :]
        return tuple(pack_edges(list(packed), halves, j, lane))

    packed = lax.fori_loop(
        0, NJ, step, tuple(jnp.zeros((HALF, LANES), F32) for _ in range(COMPS)), unroll=4
    )
    for c in range(COMPS):
        edge_ref[c] = packed[c]
        slab_ref[c] = v_ref[c, 0]


def mirror_rows(slab_ref, before_ref, after_ref, out_ref):
    for c in range(COMPS):
        out_ref[c, 0:1] = after_ref[c, 0:1]
        for i in range(ROWS):
            out_ref[c, i + 1 : i + 2] = slab_ref[c, ROWS - 1 - i : ROWS - i]
        out_ref[c, ROWS + 1 : ROWS + 2] = before_ref[c, 0:1]
        out_ref[c, ROWS + 2 :] = jnp.zeros((24 - ROWS - 2, LANES), F32)


CHUNK = 4
CHUNKS = NJ // CHUNK
AHEAD = 3


def apply_blocks(stage, *refs):
    last = stage == 2
    (v_ref, slab_ref, jac_ref, src_ref, dis_ref, before_ref, after_ref, down_ref, up_ref) = refs[:9]
    if stage == 0:
        out_ref, part_ref, low_ref, high_ref, edge_ref, wide_ref, base_ref = refs[9:16]
        q_ref, narrow_ref, sems = refs[16:]
    elif stage == 1:
        out_ref, part_ref, low_ref, high_ref, edge_ref, q_ref = refs[9:]
    else:
        far_ref, part_ref, final_ref, q_ref, out_ref, sems = refs[9:]

    def block_copy(n):
        at = pl.ds(n * CHUNK, CHUNK)
        return pltpu.make_async_copy(
            jac_ref.at[:, :, :, at], narrow_ref.at[:, :, :, at], sems.at[n]
        )

    def result_copy(n):
        at = pl.ds(n * CHUNK, CHUNK)
        return pltpu.make_async_copy(out_ref.at[:, at], far_ref.at[:, at], sems.at[n])

    if stage == 0:
        for n in range(AHEAD):
            block_copy(n).start()
    if last:
        final_copies = (
            pltpu.make_async_copy(v_ref.at[:, 1:NJ], final_ref.at[:, 1:], sems.at[CHUNKS]),
            pltpu.make_async_copy(slab_ref, final_ref.at[:, 0], sems.at[CHUNKS + 1]),
        )
        for copy in final_copies:
            copy.start()
    lane, row = lane_index(), row_index()
    place = lax.axis_index("span")
    has_down, has_up = place > 0, place < SPAN - 1
    even = (lane & 1) == 0
    for c in range(COMPS):
        from_up = jnp.where(has_up, pltpu.roll(up_ref[c], LANES - 1, 1), 0.0)
        from_down = jnp.where(has_down, pltpu.roll(down_ref[c], 1, 1), 0.0)
        q_ref[c] = jnp.where(even, from_up, from_down)
        if not last:
            out_ref[c, NJ] = jnp.zeros((ROWS, LANES), F32)
    first_lane, last_lane = lane == 0, lane == LANES - 1
    first_row, last_row = row == 0, row == HALF - 1

    def cells(c, j, half):
        at = slice(half * HALF, (half + 1) * HALF)
        if isinstance(j, int) and j < 0:
            return jnp.zeros((HALF, LANES), F32)
        if isinstance(j, int) and j == 0:
            return slab_ref[c, at]
        return v_ref[c, j, at]

    def step(j, packed):
        at_row = pl.ds(j, 1)
        dis = (dis_ref[j, :HALF], dis_ref[j, HALF:])
        diffs = [[None] * COMPS for _ in range(3)]
        sums, here = [], []
        for c in range(COMPS):
            a, b = cells(c, j, 0), cells(c, j, 1)
            here.append((a, b))
            before = spread(before_ref[c, at_row])
            after = spread(after_ref[c, at_row])
            a_up, b_up = pltpu.roll(a, HALF - 1, 0), pltpu.roll(b, HALF - 1, 0)
            a_dn, b_dn = pltpu.roll(a, 1, 0), pltpu.roll(b, 1, 0)
            next_i = (jnp.where(last_row, b_up, a_up), jnp.where(last_row, after, b_up))
            prev_i = (jnp.where(first_row, before, a_dn), jnp.where(first_row, a_dn, b_dn))
            if last and isinstance(j, int) and j == NJ - 1:
                next_j = tuple(jnp.zeros((HALF, LANES), F32) for _ in range(2))
            else:
                next_j = tuple(cells(c, j + 1, half) for half in range(2))
            prev_j = tuple(cells(c, j - 1, half) for half in range(2))
            next_k, prev_k = [], []
            for half, x in enumerate((a, b)):
                edge = pltpu.roll(q_ref[c], LANES - 1 - 4 * j - 2 * half, 1)
                next_k.append(jnp.where(last_lane, edge, pltpu.roll(x, LANES - 1, 1)))
                prev_k.append(jnp.where(first_lane, edge, pltpu.roll(x, 1, 1)))
            for d, (nxt, prv) in enumerate(((next_i, prev_i), (next_j, prev_j), (next_k, prev_k))):
                diffs[d][c] = tuple(n - p for n, p in zip(nxt, prv))
            sums.append(
                tuple(
                    (next_i[half] + prev_i[half])
                    + (next_j[half] + prev_j[half])
                    + (next_k[half] + prev_k[half])
                    for half in range(2)
                )
            )
        halves = []
        weight = None if last else tuple((OMEGA / 6.0) / d for d in dis)
        for c in range(COMPS):
            acc = [jnp.zeros((HALF, LANES), F32), jnp.zeros((HALF, LANES), F32)]
            for d in range(3):
                for b in range(COMPS):
                    if stage == 0:
                        block = narrow_ref[d, c, b, j].astype(F32)
                        wide_ref[d, c, b, j] = block
                        if d == 1 and isinstance(j, int) and j == 0:
                            base_ref[c, b] = block
                    else:
                        block = jac_ref[d, c, b, j]
                    acc[0] = acc[0] + block[:HALF] * diffs[d][b][0]
                    acc[1] = acc[1] + block[HALF:] * diffs[d][b][1]
            rest = []
            for half in range(2):
                x, total = here[c][half], sums[c][half]
                rhs = src_ref[c, j, half * HALF : (half + 1) * HALF] - acc[half]
                if last:
                    rest.append(rhs - dis[half] * (6.0 * x - total))
                else:
                    rest.append(
                        ((1.0 - OMEGA) * x + (OMEGA / 6.0) * total) + weight[half] * rhs
                    )
            if isinstance(j, int) and j == 0:
                part_ref[c, :HALF] = rest[0]
                part_ref[c, HALF:] = rest[1]
            out_ref[c, j, :HALF] = rest[0]
            out_ref[c, j, HALF:] = rest[1]
            if not last:
                low_ref[c, at_row] = rest[0][:1]
                high_ref[c, at_row] = rest[1][HALF - 1 :]
            halves.append(rest)
        if last:
            return packed
        return tuple(pack_edges(list(packed), halves, j, lane))

    def loop_step(j, packed):
        if stage == 0:

            @pl.when(j % CHUNK == 0)
            def _():
                n = j // CHUNK
                block_copy(n).wait()

                @pl.when(n + AHEAD < CHUNKS)
                def _():
                    block_copy(n + AHEAD).start()

        packed = step(j, packed)
        if last:

            @pl.when(j % CHUNK == CHUNK - 1)
            def _():
                result_copy(j // CHUNK).start()

        return packed

    packed = () if last else tuple(jnp.zeros((HALF, LANES), F32) for _ in range(COMPS))
    if stage == 0:
        block_copy(0).wait()
        block_copy(AHEAD).start()
    packed = step(0, packed)
    packed = step(1, packed)
    packed = lax.fori_loop(2, NJ, loop_step, packed)
    if last:
        for n in range(CHUNKS):
            result_copy(n).wait()
        for copy in final_copies:
            copy.wait()
    else:
        for c in range(COMPS):
            edge_ref[c] = packed[c]


def add_ghosts(last, *refs):
    (slab_ref, base_ref, dis_ref, wall_ref, partner_ref, window_ref, part_ref) = refs[:7]
    if last:
        _, far_ref, out_ref, sem = refs[7:]
    else:
        low_in, high_in, edge_in, out_ref, low_ref, high_ref, edge_ref = refs[7:]
        low_ref[...] = low_in[...]
        high_ref[...] = high_in[...]
    lane = lane_index()
    base = lax.axis_index("wrap") * ROWS
    row = lax.broadcasted_iota(jnp.int32, (ROWS, LANES), 0)
    shift = partner_ref[...] - (WRAP * ROWS - 1 - base - row)
    wall = wall_ref[...] == 1
    dis = dis_ref[0]
    ghosts = []
    for c in range(COMPS):
        rows = window_ref[c]
        lower, middle, upper = rows[:ROWS], rows[1 : ROWS + 1], rows[2 : ROWS + 2]
        chosen = jnp.where(shift == -1, upper, jnp.where(shift == 1, lower, middle))
        ghosts.append(jnp.where(wall, slab_ref[c], chosen))
    if not last:
        weight = (OMEGA / 6.0) / dis
    for c in range(COMPS):
        total = base_ref[c, 0] * ghosts[0]
        for b in range(1, COMPS):
            total = total + base_ref[c, b] * ghosts[b]
        if last:
            fresh = part_ref[c] + (dis * ghosts[c] + total)
        else:
            fresh = part_ref[c] + ((OMEGA / 6.0) * ghosts[c] + weight * total)
        out_ref[c] = fresh
        if not last:
            low_ref[c, 0:1] = fresh[:1]
            high_ref[c, 0:1] = fresh[ROWS - 1 :]
            edge = jnp.where(lane < 2, pltpu.roll(fresh[:HALF], 1, 1), edge_in[c])
            here = (lane == 2) | (lane == 3)
            edge_ref[c] = jnp.where(here, pltpu.roll(fresh[HALF:], 3, 1), edge)
    if last:
        copy = pltpu.make_async_copy(out_ref, far_ref.at[:, 0], sem)
        copy.start()
        copy.wait()


POINT_LANES = 64


def surface_sums(*refs):
    slab_ref, slope_ref, wall_ref, points_ref, weights_ref = refs[:5]
    kept_ref, sent_ref, left_ref, right_ref, sum_ref = refs[5:]
    wall = wall_ref[...].astype(F32)
    grads = []
    for x in range(3):
        total = slope_ref[x, 0] * slab_ref[0]
        for a in range(1, COMPS):
            total = total + slope_ref[x, a] * slab_ref[a]
        grads.append(total * wall)
    owner = lax.broadcasted_iota(jnp.int32, (WRAP, LANES), 0)
    inner = lax.broadcasted_iota(jnp.int32, (POINT_LANES, LANES), 0)
    for slot in range(LISTS):
        points = points_ref[slot]
        scale = weights_ref[slot]
        major, minor = points >> 6, points & (POINT_LANES - 1)
        parts = []
        for x in range(3):
            value = grads[x] * scale
            high = value.astype(BF16).astype(F32)
            parts.append((high, value - high))
        for i in range(ROWS):
            at = pl.ds((slot * ROWS + i) * LANES, LANES)
            mine = owner == jnp.broadcast_to(major[i : i + 1], (WRAP, LANES))
            for x in range(3):
                for part in range(2):
                    value = jnp.broadcast_to(parts[x][part][i : i + 1], (WRAP, LANES))
                    left_ref[x * 2 + part, :, at] = jnp.where(mine, value, 0.0).astype(BF16)
            same = inner == jnp.broadcast_to(minor[i : i + 1], (POINT_LANES, LANES))
            right_ref[:, at] = jnp.where(same, 1.0, 0.0).astype(BF16)
    left = left_ref[...].reshape(6 * WRAP, LISTS * ROWS * LANES)
    product = lax.dot_general(
        left, right_ref[...], (((1,), (1,)), ((), ())), preferred_element_type=F32
    )
    sum_ref[...] = jnp.zeros_like(sum_ref)
    for x in range(3):
        first = product[2 * x * WRAP : (2 * x + 1) * WRAP]
        second = product[(2 * x + 1) * WRAP : (2 * x + 2) * WRAP]
        both = first + second
        for w in range(WRAP):
            sum_ref[w, x : x + 1, :POINT_LANES] = both[w : w + 1]
    mine = lax.axis_index("wrap") & 1
    for n in range(WRAP // 2):
        kept_ref[n] = sum_ref[2 * n + mine]
        sent_ref[n] = sum_ref[2 * n + 1 - mine]


def halve(bit, kept_in, got_ref, kept_ref, sent_ref, sum_ref):
    sum_ref[...] = kept_in[...] + got_ref[...]
    mine = (lax.axis_index("wrap") >> bit) & 1
    for n in range(kept_ref.shape[0]):
        kept_ref[n] = sum_ref[2 * n + mine]
        sent_ref[n] = sum_ref[2 * n + 1 - mine]


def add_tiles(a_ref, b_ref, out_ref):
    out_ref[...] = a_ref[...] + b_ref[...]


def finish_points(a_ref, b_ref, out_ref):
    total = a_ref[0] + b_ref[0]
    out_ref[...] = pltpu.roll(total, LANES - 8 * lax.axis_index("span"), 1)[:3, :8]


def reduce_points(kept, sent):
    for bit in range(4):
        got = lax.ppermute(sent, "wrap", [(i, i ^ (1 << bit)) for i in range(WRAP)])
        count = kept.shape[0]
        if bit < 3:
            kept, sent = run_kernel(
                functools.partial(halve, bit + 1),
                [shape_of(count // 2, HALF, LANES)] * 2,
                (kept, got),
                scratch=(pltpu.VMEM((count, HALF, LANES), F32),),
                name="halve",
            )
        else:
            (kept,) = run_kernel(add_tiles, [shape_of(1, HALF, LANES)], (kept, got), name="add")
    for bit in range(3):
        got = lax.ppermute(kept, "span", [(i, i ^ (1 << bit)) for i in range(SPAN)])
        if bit < 2:
            (kept,) = run_kernel(add_tiles, [shape_of(1, HALF, LANES)], (kept, got), name="add")
    (out,) = run_kernel(finish_points, [shape_of(3, 8)], (kept, got), name="points")
    return out


WRAP_UP = [(i, (i + 1) % WRAP) for i in range(WRAP)]
WRAP_DOWN = [(b, a) for a, b in WRAP_UP]
SPAN_UP = [(i, (i + 1) % SPAN) for i in range(SPAN)]
SPAN_DOWN = [(b, a) for a, b in SPAN_UP]
MIRROR = [(i, WRAP - 1 - i) for i in range(WRAP)]

FIELD = (COMPS, NJ, ROWS, LANES)
TALL = (COMPS, NJ + 1, ROWS, LANES)
SLAB = (COMPS, ROWS, LANES)
FACE = (COMPS, NJ, LANES)
EDGE = (COMPS, HALF, LANES)
BLOCKS = (3, COMPS, COMPS, NJ, ROWS, LANES)
SWEEP_FLOPS = 160 * COMPS * NJ * ROWS * LANES
DMA = pltpu.SemaphoreType.DMA


def exchange(slab, low, high, edge):
    before = lax.ppermute(high, "wrap", WRAP_UP)
    after = lax.ppermute(low, "wrap", WRAP_DOWN)
    down = lax.ppermute(edge, "span", SPAN_UP)
    up = lax.ppermute(edge, "span", SPAN_DOWN)
    (rows,) = run_kernel(
        mirror_rows, [shape_of(COMPS, 24, LANES)], (slab, before, after), name="mirror"
    )
    window = lax.ppermute(rows, "wrap", MIRROR)
    return (before, after, down, up), window


def operator_step(stage, v, slab, faces, blocks, base, fixed):
    source, dissipation, wall, partner = fixed
    halos, window = exchange(slab, *faces)
    args = (v, slab, blocks, source, dissipation, *halos)
    kernel = functools.partial(apply_blocks, stage)
    if stage < 2:
        outs = [shape_of(*d) for d in (TALL, SLAB, FACE, FACE, EDGE)]
        scratch = [pltpu.VMEM(EDGE, F32)]
        if stage == 0:
            outs += [shape_of(*BLOCKS), shape_of(*BLOCKS[1:3], ROWS, LANES)]
            scratch += [pltpu.VMEM(BLOCKS, BF16), DMA((CHUNKS,))]
        v, part, *rest = run_kernel(
            kernel,
            outs,
            args,
            scratch=scratch,
            flops=SWEEP_FLOPS,
            name="blocks",
            far=(2,) if stage == 0 else (),
            vmem=12 if stage == 0 else 4,
        )
        if stage == 0:
            *rest, blocks, base = rest
        slab, *faces = run_kernel(
            functools.partial(add_ghosts, False),
            [shape_of(*d) for d in (SLAB, FACE, FACE, EDGE)],
            (slab, base, dissipation, wall, partner, window, part, *rest),
            flops=1000000,
            name="ghosts",
        )
        return v, slab, faces, blocks, base
    residual, part, final = run_kernel(
        kernel,
        [shape_of(*FIELD), shape_of(*SLAB), shape_of(*FIELD)],
        args,
        scratch=(pltpu.VMEM(EDGE, F32), pltpu.VMEM(FIELD, F32), DMA((CHUNKS + 2,))),
        flops=SWEEP_FLOPS,
        name="blocks",
        far_out=(0, 2),
    )
    (residual,) = run_kernel(
        functools.partial(add_ghosts, True),
        [shape_of(*FIELD)],
        (slab, base, dissipation, wall, partner, window, part, residual),
        scratch=(pltpu.VMEM(SLAB, F32), DMA),
        aliases={7: 0},
        flops=1000000,
        name="ghosts",
        far=(7,),
        far_out=(0,),
    )
    return final, residual


def shards(
    adjoint_start,
    adjoint_source,
    jacobians,
    dissipation,
    wall_mask,
    wake_partner,
    surface_slopes,
    control_points,
    control_weights,
):
    fixed = (adjoint_source, dissipation, wall_mask, wake_partner)
    v, slab, *faces = run_kernel(
        first_faces,
        [shape_of(*d) for d in (TALL, SLAB, FACE, FACE, EDGE)],
        (pltpu.with_memory_space_constraint(adjoint_start, pltpu.HBM),),
        scratch=(DMA,),
        flops=1000000,
        name="faces",
        far=(0,),
    )
    blocks, base = pltpu.with_memory_space_constraint(jacobians, pltpu.HBM), None
    for stage in range(2):
        v, slab, faces, blocks, base = operator_step(stage, v, slab, faces, blocks, base, fixed)
    kept, sent = run_kernel(
        surface_sums,
        [shape_of(WRAP // 2, HALF, LANES)] * 2,
        (slab, surface_slopes, wall_mask, control_points, control_weights),
        scratch=(
            pltpu.VMEM((6, WRAP, LISTS * ROWS * LANES), BF16),
            pltpu.VMEM((POINT_LANES, LISTS * ROWS * LANES), BF16),
            pltpu.VMEM((WRAP, HALF, LANES), F32),
        ),
        flops=10000000,
        name="surface",
        vmem=8,
    )
    shape_gradient = reduce_points(kept, sent)
    final, residual = operator_step(2, v, slab, faces, blocks, base, fixed)
    return final, residual, shape_gradient


def solution(mesh):
    in_specs = (
        P(None, None, "wrap", "span"),
        P(None, None, "wrap", "span"),
        P(None, None, None, None, "wrap", "span"),
        P(None, "wrap", "span"),
        P("wrap", "span"),
        P("wrap", "span"),
        P(None, None, "wrap", "span"),
        P(None, "wrap", "span"),
        P(None, "wrap", "span"),
    )
    out_specs = (
        P(None, None, "wrap", "span"),
        P(None, None, "wrap", "span"),
        P(None, ("wrap", "span")),
    )
    return jax.shard_map(shards, mesh=mesh, in_specs=in_specs, out_specs=out_specs, check_vma=False)
```

profile of v0, /device:TPU:0, one launch (start us, length us, event | category | flops | bytes accessed | tf_op | source)
XLA Modules:
  0.0 97.5 jit_solution(15525135613006013723)
XLA Ops:
  0.7 2.4 %faces.1 = (f32[5,33,16,128]{3,2,1,0:T(8,128)S(1)}, f32[5,16,128]{2,1,0:T(8,128)S(1)}, f32[5,32,128]{2,1,0:T(8,128)S(1)}, f32[5,32,128]{2,1,0:T(8,128)S(1)}, f32[5,8,128]{2,1,0:T(8,128)S(1)}) custom-call(f32[5,32,16,128]{3,2,1,0:T(8,128)} %start_ref.1), custom_call_target="tpu_custom_call" | custom-call | flops 1000000 | bytes 1310720 | tf_op jit(solution)/shard_map/faces/pallas_call | solution.py:44
  3.0 0.1 collective-permute-start
  3.1 4.7 %collective-permute-start.1 = (f32[5,32,128]{2,1,0:T(8,128)S(1)}, f32[5,32,128]{2,1,0:T(8,128)S(1)}, u32[]{:S(2)}, u32[]{:S(2)}) collective-permute-start(f32[5,32,128]{2,1,0:T(8,128)S(1)} %get-tuple-element.42), channel_id=1, source_target_pairs={{8,0},{16,8},{24,16},{32,24},{40,32},{48,40},{56,48},{64,56},{72,6... | collective-permute-start | bytes 245768 | tf_op jit(solution)/shard_map/ppermute | solution.py:427
  7.8 2.0 %collective-permute-done.refs_5_.before_ref = f32[5,32,128]{2,1,0:T(8,128)S(1)} collective-permute-done((f32[5,32,128]{2,1,0:T(8,128)S(1)}, f32[5,32,128]{2,1,0:T(8,128)S(1)}, u32[]{:S(2)}, u32[]{:S(2)}) %collective-permute-start) | collective-permute-done | bytes 81952 | tf_op jit(solution)/shard_map/ppermute | solution.py:426
  9.8 0.0 collective-permute-done.1.refs_6_.after_ref
  9.9 4.0 %collective-permute-start.4 = (f32[5,24,128]{2,1,0:T(8,128)S(1)}, f32[5,24,128]{2,1,0:T(8,128)S(1)}, u32[]{:S(2)}, u32[]{:S(2)}) collective-permute-start(f32[5,24,128]{2,1,0:T(8,128)S(1)} %mirror.3), channel_id=1, source_target_pairs={{0,120},{8,112},{16,104},{24,96},{32,88},{40,80},{48,72},{56,64},{... | collective-permute-start | bytes 184328 | tf_op jit(solution)/shard_map/ppermute | solution.py:433
  13.9 2.9 %collective-permute-start.2 = (f32[5,8,128]{2,1,0:T(8,128)S(1)}, f32[5,8,128]{2,1,0:T(8,128)S(1)}, u32[]{:S(2)}, u32[]{:S(2)}) collective-permute-start(f32[5,8,128]{2,1,0:T(8,128)S(1)} %get-tuple-element.43), channel_id=1, source_target_pairs={{0,1},{1,2},{2,3},{3,4},{4,5},{5,6},{6,7},{7,0},{8,9},{9,10},{10,1... | collective-permute-start | bytes 61448 | tf_op jit(solution)/shard_map/ppermute | solution.py:428
  16.8 2.7 %collective-permute-start.3 = (f32[5,8,128]{2,1,0:T(8,128)S(1)}, f32[5,8,128]{2,1,0:T(8,128)S(1)}, u32[]{:S(2)}, u32[]{:S(2)}) collective-permute-start(f32[5,8,128]{2,1,0:T(8,128)S(1)} %get-tuple-element.43), channel_id=1, source_target_pairs={{1,0},{2,1},{3,2},{4,3},{5,4},{6,5},{7,6},{0,7},{9,8},{10,9},{11,1... | collective-permute-start | bytes 61448 | tf_op jit(solution)/shard_map/ppermute | solution.py:429
  19.5 1.8 %collective-permute-done.2.refs_7_ = f32[5,8,128]{2,1,0:T(8,128)S(1)} collective-permute-done((f32[5,8,128]{2,1,0:T(8,128)S(1)}, f32[5,8,128]{2,1,0:T(8,128)S(1)}, u32[]{:S(2)}, u32[]{:S(2)}) %collective-permute-start.2) | collective-permute-done | bytes 20512 | tf_op jit(solution)/shard_map/ppermute | solution.py:428
  21.3 0.8 collective-permute-done.3.refs_8_
  22.1 8.1 %blocks.3 = (f32[5,33,16,128]{3,2,1,0:T(8,128)S(1)}, f32[5,16,128]{2,1,0:T(8,128)S(1)}, f32[5,32,128]{2,1,0:T(8,128)S(1)}, f32[5,32,128]{2,1,0:T(8,128)S(1)}, f3...) custom-call(f32[5,33,16,128]{3,2,1,0:T(8,128)S(1)} %get-tuple-element.39.refs_0_, ...), custom_call_target="tpu_custom_call" | custom-call | flops 52428800 | bytes 13000704 | tf_op jit(solution)/shard_map/blocks/pallas_call | solution.py:44
  30.2 0.0 collective-permute-done.4.refs_5_
  30.2 0.1 ghosts.3
  30.3 0.1 collective-permute-start.5
  30.4 3.8 %collective-permute-start.6 = (f32[5,32,128]{2,1,0:T(8,128)S(1)}, f32[5,32,128]{2,1,0:T(8,128)S(1)}, u32[]{:S(2)}, u32[]{:S(2)}) collective-permute-start(f32[5,32,128]{2,1,0:T(8,128)S(1)} %get-tuple-element.53), channel_id=1, source_target_pairs={{8,0},{16,8},{24,16},{32,24},{40,32},{48,40},{56,48},{64,56},{72,6... | collective-permute-start | bytes 245768 | tf_op jit(solution)/shard_map/ppermute | solution.py:427
  34.2 2.1 %collective-permute-done.5.refs_5_.before_ref = f32[5,32,128]{2,1,0:T(8,128)S(1)} collective-permute-done((f32[5,32,128]{2,1,0:T(8,128)S(1)}, f32[5,32,128]{2,1,0:T(8,128)S(1)}, u32[]{:S(2)}, u32[]{:S(2)}) %collective-permute-start.5) | collective-permute-done | bytes 81952 | tf_op jit(solution)/shard_map/ppermute | solution.py:426
  36.3 0.0 collective-permute-done.6.refs_6_.after_ref
  36.4 4.4 %collective-permute-start.9 = (f32[5,24,128]{2,1,0:T(8,128)S(1)}, f32[5,24,128]{2,1,0:T(8,128)S(1)}, u32[]{:S(2)}, u32[]{:S(2)}) collective-permute-start(f32[5,24,128]{2,1,0:T(8,128)S(1)} %mirror.4), channel_id=1, source_target_pairs={{0,120},{8,112},{16,104},{24,96},{32,88},{40,80},{48,72},{56,64},{... | collective-permute-start | bytes 184328 | tf_op jit(solution)/shard_map/ppermute | solution.py:433
  40.8 2.5 %collective-permute-start.7 = (f32[5,8,128]{2,1,0:T(8,128)S(1)}, f32[5,8,128]{2,1,0:T(8,128)S(1)}, u32[]{:S(2)}, u32[]{:S(2)}) collective-permute-start(f32[5,8,128]{2,1,0:T(8,128)S(1)} %get-tuple-element.54), channel_id=1, source_target_pairs={{0,1},{1,2},{2,3},{3,4},{4,5},{5,6},{6,7},{7,0},{8,9},{9,10},{10,1... | collective-permute-start | bytes 61448 | tf_op jit(solution)/shard_map/ppermute | solution.py:428
  43.2 3.2 %collective-permute-start.8 = (f32[5,8,128]{2,1,0:T(8,128)S(1)}, f32[5,8,128]{2,1,0:T(8,128)S(1)}, u32[]{:S(2)}, u32[]{:S(2)}) collective-permute-start(f32[5,8,128]{2,1,0:T(8,128)S(1)} %get-tuple-element.54), channel_id=1, source_target_pairs={{1,0},{2,1},{3,2},{4,3},{5,4},{6,5},{7,6},{0,7},{9,8},{10,9},{11,1... | collective-permute-start | bytes 61448 | tf_op jit(solution)/shard_map/ppermute | solution.py:429
  46.4 1.8 %collective-permute-done.7.refs_7_ = f32[5,8,128]{2,1,0:T(8,128)S(1)} collective-permute-done((f32[5,8,128]{2,1,0:T(8,128)S(1)}, f32[5,8,128]{2,1,0:T(8,128)S(1)}, u32[]{:S(2)}, u32[]{:S(2)}) %collective-permute-start.7) | collective-permute-done | bytes 20512 | tf_op jit(solution)/shard_map/ppermute | solution.py:428
  48.2 0.3 collective-permute-done.8.refs_8_
  48.5 6.0 %blocks.4 = (f32[5,33,16,128]{3,2,1,0:T(8,128)S(1)}, f32[5,16,128]{2,1,0:T(8,128)S(1)}, f32[5,32,128]{2,1,0:T(8,128)S(1)}, f32[5,32,128]{2,1,0:T(8,128)S(1)}, f32[5,8,128]{2,1,0:T(8,128)S(1)}) custom-call(f32[5,33,16,128]{3,2,1,0:T(8,128)S(1)} %get-tuple-element.44.refs_0_, f32[5,16,128]{2,1,0:T(8,128)S(1)} %get-tuple-element.50.refs_1_.slab_ref.refs_0_, ...), custom_call_target="tpu_custom_call" | custom-call | flops 52428800 | bytes 22831104 | tf_op jit(solution)/shard_map/blocks/pallas_call | solution.py:44
  54.5 0.0 collective-permute-done.9.refs_5_
  54.5 0.1 ghosts.4
  54.6 0.1 collective-permute-start.10
  54.7 3.8 %collective-permute-start.11 = (f32[5,32,128]{2,1,0:T(8,128)S(1)}, f32[5,32,128]{2,1,0:T(8,128)S(1)}, u32[]{:S(2)}, u32[]{:S(2)}) collective-permute-start(f32[5,32,128]{2,1,0:T(8,128)S(1)} %get-tuple-element.62), channel_id=1, source_target_pairs={{8,0},{16,8},{24,16},{32,24},{40,32},{48,40},{56,48},{64,56},{72,6... | collective-permute-start | bytes 245768 | tf_op jit(solution)/shard_map/ppermute | solution.py:427
  58.6 1.1 %surface.1 = (f32[8,8,128]{2,1,0:T(8,128)S(1)}, f32[8,8,128]{2,1,0:T(8,128)S(1)}) custom-call(f32[5,16,128]{2,1,0:T(8,128)S(1)} %get-tuple-element.60.refs_1_.slab_ref.refs_0_, f32[3,5,16,128]{3,2,1,0:T(8,128)S(1)} %copy-done.3, s32[16,128]{1,0:T(8,128)S(1)} %copy-done.2, s32[4,16,128]{2,1,0:T(8,128)S(1)} %copy-done.5, f32[4,16,128]{2,1,0:T(8,128)S(1)} %copy-done.6), custom_call_target="tpu_custom_call" | custom-call | flops 10000000 | bytes 237568 | tf_op jit(solution)/shard_map/surface/pallas_call | solution.py:44
  59.7 0.1 collective-permute-start.15
  59.8 0.9 collective-permute-done.10.refs_5_.before_ref
  60.7 0.0 collective-permute-done.11.refs_6_.after_ref
  60.7 3.9 %collective-permute-start.14 = (f32[5,24,128]{2,1,0:T(8,128)S(1)}, f32[5,24,128]{2,1,0:T(8,128)S(1)}, u32[]{:S(2)}, u32[]{:S(2)}) collective-permute-start(f32[5,24,128]{2,1,0:T(8,128)S(1)} %mirror.5), channel_id=1, source_target_pairs={{0,120},{8,112},{16,104},{24,96},{32,88},{40,80},{48,72},{56,64},{... | collective-permute-start | bytes 184328 | tf_op jit(solution)/shard_map/ppermute | solution.py:433
  64.7 0.1 collective-permute-start.16
  64.8 3.7 %collective-permute-done.16.got_ref = f32[4,8,128]{2,1,0:T(8,128)S(1)} collective-permute-done((f32[4,8,128]{2,1,0:T(8,128)S(1)}, f32[4,8,128]{2,1,0:T(8,128)S(1)}, u32[]{:S(2)}, u32[]{:S(2)}) %collective-permute-start.16) | collective-permute-done | bytes 16416 | tf_op jit(solution)/shard_map/ppermute | solution.py:389
  68.5 3.0 %collective-permute-start.12 = (f32[5,8,128]{2,1,0:T(8,128)S(1)}, f32[5,8,128]{2,1,0:T(8,128)S(1)}, u32[]{:S(2)}, u32[]{:S(2)}) collective-permute-start(f32[5,8,128]{2,1,0:T(8,128)S(1)} %get-tuple-element.63), channel_id=1, source_target_pairs={{0,1},{1,2},{2,3},{3,4},{4,5},{5,6},{6,7},{7,0},{8,9},{9,10},{10,1... | collective-permute-start | bytes 61448 | tf_op jit(solution)/shard_map/ppermute | solution.py:428
  71.5 2.7 %collective-permute-start.13 = (f32[5,8,128]{2,1,0:T(8,128)S(1)}, f32[5,8,128]{2,1,0:T(8,128)S(1)}, u32[]{:S(2)}, u32[]{:S(2)}) collective-permute-start(f32[5,8,128]{2,1,0:T(8,128)S(1)} %get-tuple-element.63), channel_id=1, source_target_pairs={{1,0},{2,1},{3,2},{4,3},{5,4},{6,5},{7,6},{0,7},{9,8},{10,9},{11,1... | collective-permute-start | bytes 61448 | tf_op jit(solution)/shard_map/ppermute | solution.py:429
  74.2 0.0 collective-permute-done.17.got_ref
  74.2 0.9 collective-permute-start.18
  75.2 2.7 %collective-permute-done.18.b_ref = f32[1,8,128]{2,1,0:T(8,128)S(1)} collective-permute-done((f32[1,8,128]{2,1,0:T(8,128)S(1)}, f32[1,8,128]{2,1,0:T(8,128)S(1)}, u32[]{:S(2)}, u32[]{:S(2)}) %collective-permute-start.18) | collective-permute-done | bytes 4128 | tf_op jit(solution)/shard_map/ppermute | solution.py:389
  77.9 2.3 %collective-permute-start.19 = (f32[1,8,128]{2,1,0:T(8,128)S(1)}, f32[1,8,128]{2,1,0:T(8,128)S(1)}, u32[]{:S(2)}, u32[]{:S(2)}) collective-permute-start(f32[1,8,128]{2,1,0:T(8,128)S(1)} %add.3.a_ref), channel_id=1, source_target_pairs={{0,1},{1,0},{2,3},{3,2},{4,5},{5,4},{6,7},{7,6},{8,9},{9,8},{10,11... | collective-permute-start | bytes 12296 | tf_op jit(solution)/shard_map/ppermute | solution.py:402
  80.2 2.8 %collective-permute-done.19.b_ref = f32[1,8,128]{2,1,0:T(8,128)S(1)} collective-permute-done((f32[1,8,128]{2,1,0:T(8,128)S(1)}, f32[1,8,128]{2,1,0:T(8,128)S(1)}, u32[]{:S(2)}, u32[]{:S(2)}) %collective-permute-start.19) | collective-permute-done | bytes 4128 | tf_op jit(solution)/shard_map/ppermute | solution.py:402
  83.0 0.9 collective-permute-start.20
  83.9 2.7 %collective-permute-done.20.b_ref = f32[1,8,128]{2,1,0:T(8,128)S(1)} collective-permute-done((f32[1,8,128]{2,1,0:T(8,128)S(1)}, f32[1,8,128]{2,1,0:T(8,128)S(1)}, u32[]{:S(2)}, u32[]{:S(2)}) %collective-permute-start.20) | collective-permute-done | bytes 4128 | tf_op jit(solution)/shard_map/ppermute | solution.py:402
  86.6 2.1 %collective-permute-start.21 = (f32[1,8,128]{2,1,0:T(8,128)S(1)}, f32[1,8,128]{2,1,0:T(8,128)S(1)}, u32[]{:S(2)}, u32[]{:S(2)}) collective-permute-start(f32[1,8,128]{2,1,0:T(8,128)S(1)} %add.5.a_ref), channel_id=1, source_target_pairs={{0,4},{1,5},{2,6},{3,7},{4,0},{5,1},{6,2},{7,3},{8,12},{9,13},{10,... | collective-permute-start | bytes 12296 | tf_op jit(solution)/shard_map/ppermute | solution.py:402
  88.7 3.0 %collective-permute-done.21.b_ref = f32[1,8,128]{2,1,0:T(8,128)S(1)} collective-permute-done((f32[1,8,128]{2,1,0:T(8,128)S(1)}, f32[1,8,128]{2,1,0:T(8,128)S(1)}, u32[]{:S(2)}, u32[]{:S(2)}) %collective-permute-start.21) | collective-permute-done | bytes 4128 | tf_op jit(solution)/shard_map/ppermute | solution.py:402
  91.7 0.6 points.1
  92.4 4.4 %blocks.5 = (f32[5,32,16,128]{3,2,1,0:T(8,128)}, f32[5,16,128]{2,1,0:T(8,128)S(1)}, f32[5,32,16,128]{3,2,1,0:T(8,128)}) custom-call(f32[5,33,16,128]{3,2,1,0:T(8,128)S(1)} %get-tuple-element.55.refs_0_, f32[5,16,128]{2,1,0:T(8,128)S(1)} %get-tuple-element.60.refs_1_.slab_ref.refs_0_, f32[3,5,5,32,16,128]{5,4,3,2,1,0:T(8,128)S(1)} %get-tuple-element.51.refs_2_, ...), custom_call_target="tpu_custom_call" | custom-call | flops 52428800 | bytes 22831104 | tf_op jit(solution)/shard_map/blocks/pallas_call | solution.py:44
  96.8 0.7 ghosts.5
  (28 shorter events, 0.2 us)
Async XLA Ops:
  0.6 21.4 %copy-start = (f32[5,32,16,128]{3,2,1,0:T(8,128)S(1)}, f32[5,32,16,128]{3,2,1,0:T(8,128)}, u32[]{:S(2)}) copy-start(f32[5,32,16,128]{3,2,1,0:T(8,128)} %refs_3_.11) | copy-start | bytes 3932164
  0.6 21.4 %copy-start.1 = (f32[32,16,128]{2,1,0:T(8,128)S(1)}, f32[32,16,128]{2,1,0:T(8,128)}, u32[]{:S(2)}) copy-start(f32[32,16,128]{2,1,0:T(8,128)} %refs_2_.8) | copy-start | bytes 786436
  3.0 6.8 %collective-permute-start = (f32[5,32,128]{2,1,0:T(8,128)S(1)}, f32[5,32,128]{2,1,0:T(8,128)S(1)}, u32[]{:S(2)}, u32[]{:S(2)}) collective-permute-start(f32[5,32,128]{2,1,0:T(8,128)S(1)} %get-tuple-element.41), channel_id=1, source_target_pairs={{0,8},{8,16},{16,24},{24,32},{32,40},{40,48},{48,56},{56,64},{64,7... | collective-permute-start | bytes 245768 | tf_op jit(solution)/shard_map/ppermute | solution.py:426
  3.1 6.7 %collective-permute-start.1 = (f32[5,32,128]{2,1,0:T(8,128)S(1)}, f32[5,32,128]{2,1,0:T(8,128)S(1)}, u32[]{:S(2)}, u32[]{:S(2)}) collective-permute-start(f32[5,32,128]{2,1,0:T(8,128)S(1)} %get-tuple-element.42), channel_id=1, source_target_pairs={{8,0},{16,8},{24,16},{32,24},{40,32},{48,40},{56,48},{64,56},{72,6... | collective-permute-start | bytes 245768 | tf_op jit(solution)/shard_map/ppermute | solution.py:427
  9.9 20.3 %collective-permute-start.4 = (f32[5,24,128]{2,1,0:T(8,128)S(1)}, f32[5,24,128]{2,1,0:T(8,128)S(1)}, u32[]{:S(2)}, u32[]{:S(2)}) collective-permute-start(f32[5,24,128]{2,1,0:T(8,128)S(1)} %mirror.3), channel_id=1, source_target_pairs={{0,120},{8,112},{16,104},{24,96},{32,88},{40,80},{48,72},{56,64},{... | collective-permute-start | bytes 184328 | tf_op jit(solution)/shard_map/ppermute | solution.py:433
  13.9 7.4 %collective-permute-start.2 = (f32[5,8,128]{2,1,0:T(8,128)S(1)}, f32[5,8,128]{2,1,0:T(8,128)S(1)}, u32[]{:S(2)}, u32[]{:S(2)}) collective-permute-start(f32[5,8,128]{2,1,0:T(8,128)S(1)} %get-tuple-element.43), channel_id=1, source_target_pairs={{0,1},{1,2},{2,3},{3,4},{4,5},{5,6},{6,7},{7,0},{8,9},{9,10},{10,1... | collective-permute-start | bytes 61448 | tf_op jit(solution)/shard_map/ppermute | solution.py:428
  16.8 5.3 %collective-permute-start.3 = (f32[5,8,128]{2,1,0:T(8,128)S(1)}, f32[5,8,128]{2,1,0:T(8,128)S(1)}, u32[]{:S(2)}, u32[]{:S(2)}) collective-permute-start(f32[5,8,128]{2,1,0:T(8,128)S(1)} %get-tuple-element.43), channel_id=1, source_target_pairs={{1,0},{2,1},{3,2},{4,3},{5,4},{6,5},{7,6},{0,7},{9,8},{10,9},{11,1... | collective-permute-start | bytes 61448 | tf_op jit(solution)/shard_map/ppermute | solution.py:429
  22.1 8.1 %copy-start.2 = (s32[16,128]{1,0:T(8,128)S(1)}, s32[16,128]{1,0:T(8,128)}, u32[]{:S(2)}) copy-start(s32[16,128]{1,0:T(8,128)} %refs_2_.9) | copy-start | bytes 24580
  22.1 8.1 %copy-start.4 = (s32[16,128]{1,0:T(8,128)S(1)}, s32[16,128]{1,0:T(8,128)}, u32[]{:S(2)}) copy-start(s32[16,128]{1,0:T(8,128)} %refs_4_.12) | copy-start | bytes 24580
  30.3 6.0 %collective-permute-start.5 = (f32[5,32,128]{2,1,0:T(8,128)S(1)}, f32[5,32,128]{2,1,0:T(8,128)S(1)}, u32[]{:S(2)}, u32[]{:S(2)}) collective-permute-start(f32[5,32,128]{2,1,0:T(8,128)S(1)} %get-tuple-element.52), channel_id=1, source_target_pairs={{0,8},{8,16},{16,24},{24,32},{32,40},{40,48},{48,56},{56,64},{64,7... | collective-permute-start | bytes 245768 | tf_op jit(solution)/shard_map/ppermute | solution.py:426
  30.4 6.0 %collective-permute-start.6 = (f32[5,32,128]{2,1,0:T(8,128)S(1)}, f32[5,32,128]{2,1,0:T(8,128)S(1)}, u32[]{:S(2)}, u32[]{:S(2)}) collective-permute-start(f32[5,32,128]{2,1,0:T(8,128)S(1)} %get-tuple-element.53), channel_id=1, source_target_pairs={{8,0},{16,8},{24,16},{32,24},{40,32},{48,40},{56,48},{64,56},{72,6... | collective-permute-start | bytes 245768 | tf_op jit(solution)/shard_map/ppermute | solution.py:427
  36.4 18.1 %collective-permute-start.9 = (f32[5,24,128]{2,1,0:T(8,128)S(1)}, f32[5,24,128]{2,1,0:T(8,128)S(1)}, u32[]{:S(2)}, u32[]{:S(2)}) collective-permute-start(f32[5,24,128]{2,1,0:T(8,128)S(1)} %mirror.4), channel_id=1, source_target_pairs={{0,120},{8,112},{16,104},{24,96},{32,88},{40,80},{48,72},{56,64},{... | collective-permute-start | bytes 184328 | tf_op jit(solution)/shard_map/ppermute | solution.py:433
  40.8 7.4 %collective-permute-start.7 = (f32[5,8,128]{2,1,0:T(8,128)S(1)}, f32[5,8,128]{2,1,0:T(8,128)S(1)}, u32[]{:S(2)}, u32[]{:S(2)}) collective-permute-start(f32[5,8,128]{2,1,0:T(8,128)S(1)} %get-tuple-element.54), channel_id=1, source_target_pairs={{0,1},{1,2},{2,3},{3,4},{4,5},{5,6},{6,7},{7,0},{8,9},{9,10},{10,1... | collective-permute-start | bytes 61448 | tf_op jit(solution)/shard_map/ppermute | solution.py:428
  43.2 5.3 %collective-permute-start.8 = (f32[5,8,128]{2,1,0:T(8,128)S(1)}, f32[5,8,128]{2,1,0:T(8,128)S(1)}, u32[]{:S(2)}, u32[]{:S(2)}) collective-permute-start(f32[5,8,128]{2,1,0:T(8,128)S(1)} %get-tuple-element.54), channel_id=1, source_target_pairs={{1,0},{2,1},{3,2},{4,3},{5,4},{6,5},{7,6},{0,7},{9,8},{10,9},{11,1... | collective-permute-start | bytes 61448 | tf_op jit(solution)/shard_map/ppermute | solution.py:429
  48.5 10.0 %copy-start.3 = (f32[3,5,16,128]{3,2,1,0:T(8,128)S(1)}, f32[3,5,16,128]{3,2,1,0:T(8,128)}, u32[]{:S(2)}) copy-start(f32[3,5,16,128]{3,2,1,0:T(8,128)} %refs_1_.1) | copy-start | bytes 368644
  48.5 10.0 %copy-start.5 = (s32[4,16,128]{2,1,0:T(8,128)S(1)}, s32[4,16,128]{2,1,0:T(8,128)}, u32[]{:S(2)}) copy-start(s32[4,16,128]{2,1,0:T(8,128)} %refs_3_.13) | copy-start | bytes 98308
  48.5 10.0 %copy-start.6 = (f32[4,16,128]{2,1,0:T(8,128)S(1)}, f32[4,16,128]{2,1,0:T(8,128)}, u32[]{:S(2)}) copy-start(f32[4,16,128]{2,1,0:T(8,128)} %refs_4_.13) | copy-start | bytes 98308
  54.6 6.0 %collective-permute-start.10 = (f32[5,32,128]{2,1,0:T(8,128)S(1)}, f32[5,32,128]{2,1,0:T(8,128)S(1)}, u32[]{:S(2)}, u32[]{:S(2)}) collective-permute-start(f32[5,32,128]{2,1,0:T(8,128)S(1)} %get-tuple-element.61), channel_id=1, source_target_pairs={{0,8},{8,16},{16,24},{24,32},{32,40},{40,48},{48,56},{56,64},{64,7... | collective-permute-start | bytes 245768 | tf_op jit(solution)/shard_map/ppermute | solution.py:426
  54.7 6.0 %collective-permute-start.11 = (f32[5,32,128]{2,1,0:T(8,128)S(1)}, f32[5,32,128]{2,1,0:T(8,128)S(1)}, u32[]{:S(2)}, u32[]{:S(2)}) collective-permute-start(f32[5,32,128]{2,1,0:T(8,128)S(1)} %get-tuple-element.62), channel_id=1, source_target_pairs={{8,0},{16,8},{24,16},{32,24},{40,32},{48,40},{56,48},{64,56},{72,6... | collective-permute-start | bytes 245768 | tf_op jit(solution)/shard_map/ppermute | solution.py:427
  59.7 5.0 %collective-permute-start.15 = (f32[8,8,128]{2,1,0:T(8,128)S(1)}, f32[8,8,128]{2,1,0:T(8,128)S(1)}, u32[]{:S(2)}, u32[]{:S(2)}) collective-permute-start(f32[8,8,128]{2,1,0:T(8,128)S(1)} %get-tuple-element.68), channel_id=1, source_target_pairs={{0,8},{8,0},{16,24},{24,16},{32,40},{40,32},{48,56},{56,48},{64,72... | collective-permute-start | bytes 98312 | tf_op jit(solution)/shard_map/ppermute | solution.py:389
  60.7 36.1 %collective-permute-start.14 = (f32[5,24,128]{2,1,0:T(8,128)S(1)}, f32[5,24,128]{2,1,0:T(8,128)S(1)}, u32[]{:S(2)}, u32[]{:S(2)}) collective-permute-start(f32[5,24,128]{2,1,0:T(8,128)S(1)} %mirror.5), channel_id=1, source_target_pairs={{0,120},{8,112},{16,104},{24,96},{32,88},{40,80},{48,72},{56,64},{... | collective-permute-start | bytes 184328 | tf_op jit(solution)/shard_map/ppermute | solution.py:433
  64.7 3.8 %collective-permute-start.16 = (f32[4,8,128]{2,1,0:T(8,128)S(1)}, f32[4,8,128]{2,1,0:T(8,128)S(1)}, u32[]{:S(2)}, u32[]{:S(2)}) collective-permute-start(f32[4,8,128]{2,1,0:T(8,128)S(1)} %get-tuple-element.70), channel_id=1, source_target_pairs={{0,16},{8,24},{16,0},{24,8},{32,48},{40,56},{48,32},{56,40},{64,80... | collective-permute-start | bytes 49160 | tf_op jit(solution)/shard_map/ppermute | solution.py:389
  68.5 5.7 %collective-permute-start.17 = (f32[2,8,128]{2,1,0:T(8,128)S(1)}, f32[2,8,128]{2,1,0:T(8,128)S(1)}, u32[]{:S(2)}, u32[]{:S(2)}) collective-permute-start(f32[2,8,128]{2,1,0:T(8,128)S(1)} %get-tuple-element.72), channel_id=1, source_target_pairs={{0,32},{8,40},{16,48},{24,56},{32,0},{40,8},{48,16},{56,24},{64,96... | collective-permute-start | bytes 24584 | tf_op jit(solution)/shard_map/ppermute | solution.py:389
  68.5 23.9 %collective-permute-start.12 = (f32[5,8,128]{2,1,0:T(8,128)S(1)}, f32[5,8,128]{2,1,0:T(8,128)S(1)}, u32[]{:S(2)}, u32[]{:S(2)}) collective-permute-start(f32[5,8,128]{2,1,0:T(8,128)S(1)} %get-tuple-element.63), channel_id=1, source_target_pairs={{0,1},{1,2},{2,3},{3,4},{4,5},{5,6},{6,7},{7,0},{8,9},{9,10},{10,1... | collective-permute-start | bytes 61448 | tf_op jit(solution)/shard_map/ppermute | solution.py:428
  71.5 20.9 %collective-permute-start.13 = (f32[5,8,128]{2,1,0:T(8,128)S(1)}, f32[5,8,128]{2,1,0:T(8,128)S(1)}, u32[]{:S(2)}, u32[]{:S(2)}) collective-permute-start(f32[5,8,128]{2,1,0:T(8,128)S(1)} %get-tuple-element.63), channel_id=1, source_target_pairs={{1,0},{2,1},{3,2},{4,3},{5,4},{6,5},{7,6},{0,7},{9,8},{10,9},{11,1... | collective-permute-start | bytes 61448 | tf_op jit(solution)/shard_map/ppermute | solution.py:429
  74.2 3.7 %collective-permute-start.18 = (f32[1,8,128]{2,1,0:T(8,128)S(1)}, f32[1,8,128]{2,1,0:T(8,128)S(1)}, u32[]{:S(2)}, u32[]{:S(2)}) collective-permute-start(f32[1,8,128]{2,1,0:T(8,128)S(1)} %get-tuple-element.74), channel_id=1, source_target_pairs={{0,64},{8,72},{16,80},{24,88},{32,96},{40,104},{48,112},{56,120},{... | collective-permute-start | bytes 12296 | tf_op jit(solution)/shard_map/ppermute | solution.py:389
  77.9 5.1 %collective-permute-start.19 = (f32[1,8,128]{2,1,0:T(8,128)S(1)}, f32[1,8,128]{2,1,0:T(8,128)S(1)}, u32[]{:S(2)}, u32[]{:S(2)}) collective-permute-start(f32[1,8,128]{2,1,0:T(8,128)S(1)} %add.3.a_ref), channel_id=1, source_target_pairs={{0,1},{1,0},{2,3},{3,2},{4,5},{5,4},{6,7},{7,6},{8,9},{9,8},{10,11... | collective-permute-start | bytes 12296 | tf_op jit(solution)/shard_map/ppermute | solution.py:402
  83.0 3.6 %collective-permute-start.20 = (f32[1,8,128]{2,1,0:T(8,128)S(1)}, f32[1,8,128]{2,1,0:T(8,128)S(1)}, u32[]{:S(2)}, u32[]{:S(2)}) collective-permute-start(f32[1,8,128]{2,1,0:T(8,128)S(1)} %add.4.a_ref), channel_id=1, source_target_pairs={{0,2},{1,3},{2,0},{3,1},{4,6},{5,7},{6,4},{7,5},{8,10},{9,11},{10,... | collective-permute-start | bytes 12296 | tf_op jit(solution)/shard_map/ppermute | solution.py:402
  86.6 5.1 %collective-permute-start.21 = (f32[1,8,128]{2,1,0:T(8,128)S(1)}, f32[1,8,128]{2,1,0:T(8,128)S(1)}, u32[]{:S(2)}, u32[]{:S(2)}) collective-permute-start(f32[1,8,128]{2,1,0:T(8,128)S(1)} %add.5.a_ref), channel_id=1, source_target_pairs={{0,4},{1,5},{2,6},{3,7},{4,0},{5,1},{6,2},{7,3},{8,12},{9,13},{10,... | collective-permute-start | bytes 12296 | tf_op jit(solution)/shard_map/ppermute | solution.py:402
where the time goes:
time: 97.6 us; the launch traced here: 97.5 us
  starting transfers between devices  48.2 us (49%)
  waiting for transfers between devices  24.8 us (25%)
  Pallas kernels  23.6 us (24%)
    pallas_call x18, Pallas kernels, run_kernel(): pl.pallas_call(kernel, out_shape=outs, in_specs=[FARSPEC if n in far else...  23.6 us
    ppermute x3, starting transfers between devices, exchange(): after = lax.ppermute(low, 'wrap', WRAP_DOWN)  12.4 us
    ppermute x3, starting transfers between devices, exchange(): window = lax.ppermute(rows, 'wrap', MIRROR)  12.3 us
    ppermute x3, starting transfers between devices, exchange(): up = lax.ppermute(edge, 'span', SPAN_DOWN)  8.66 us
    ppermute x3, waiting for transfers between devices, reduce_points(): got = lax.ppermute(kept, 'span', [(i, i ^ 1 << bit) for i in range(SPAN)])  8.6 us
    ppermute x3, starting transfers between devices, exchange(): down = lax.ppermute(edge, 'span', SPAN_UP)  8.32 us
    ppermute x4, waiting for transfers between devices, reduce_points(): got = lax.ppermute(sent, 'wrap', [(i, i ^ 1 << bit) for i in range(WRAP)])  6.48 us
    ppermute x3, starting transfers between devices, reduce_points(): got = lax.ppermute(kept, 'span', [(i, i ^ 1 << bit) for i in range(SPAN)])  5.23 us
  transfers between devices with their start and end apart: 22, of which 12 were waited for; matrix products, arithmetic and copies ran while one was open for 0% of the time, Pallas kernels for 21%

commit v1 on v0

v1 whole, which is shorter than its diff:
```python
import functools

import jax
import jax.numpy as jnp
from jax import lax
from jax.experimental import pallas as pl
from jax.experimental.pallas import tpu as pltpu
from jax.sharding import PartitionSpec as P

COMPS = 5
NJ = 32
ROWS = 16
LANES = 128
HALF = 8
WRAP = 16
SPAN = 8
LISTS = 4
OMEGA = 0.8
F32 = jnp.float32
BF16 = jnp.bfloat16
VSPEC = pl.BlockSpec(memory_space=pltpu.VMEM)


def shape_of(*dims, dtype=F32):
    return jax.ShapeDtypeStruct(dims, dtype)


FARSPEC = pl.BlockSpec(memory_space=pltpu.HBM)


def run_kernel(kernel, outs, args, scratch=(), aliases=None, flops=0, far=(), far_out=(), vmem=4):
    moved = sum(a.size * a.dtype.itemsize for a in args)
    return pl.pallas_call(
        kernel,
        out_shape=outs,
        in_specs=[FARSPEC if n in far else VSPEC for n in range(len(args))],
        out_specs=[FARSPEC if n in far_out else VSPEC for n in range(len(outs))],
        scratch_shapes=list(scratch),
        input_output_aliases=aliases or {},
        compiler_params=pltpu.CompilerParams(vmem_limit_bytes=int(vmem * 2**20)),
        cost_estimate=pl.CostEstimate(flops=flops, transcendentals=0, bytes_accessed=moved),
    )(*args)


def lane_index():
    return lax.broadcasted_iota(jnp.int32, (HALF, LANES), 1)


def row_index():
    return lax.broadcasted_iota(jnp.int32, (HALF, LANES), 0)


def spread(row):
    return jnp.broadcast_to(row, (HALF, LANES))


def pack_edges(packed, halves, j, lane):
    for half in range(2):
        m = 2 * j + half
        here = (lane >> 1) == m
        for c in range(COMPS):
            packed[c] = jnp.where(here, pltpu.roll(halves[c][half], 2 * m + 1, 1), packed[c])
    return packed


def part_faces(low_ref, high_ref, pair_ref, odd_ref):
    even = (lax.axis_index("wrap") & 1) == 0
    low, high = low_ref[:COMPS], high_ref[:COMPS]
    pair_ref[...] = jnp.where(even, high, low)
    odd_ref[...] = jnp.where(even, low, high)


def first_faces(start_ref, v_ref, slab_ref, pair_ref, odd_ref, edge_ref, low_ref, high_ref, sem):
    lane = lane_index()
    copy = pltpu.make_async_copy(start_ref, v_ref.at[:, :NJ], sem)
    copy.start()
    for c in range(COMPS):
        v_ref[c, NJ] = jnp.zeros((ROWS, LANES), F32)
    copy.wait()

    def step(j, packed):
        halves = [(v_ref[c, j, :HALF], v_ref[c, j, HALF:]) for c in range(COMPS)]
        for c in range(COMPS):
            low_ref[c, pl.ds(j, 1)] = halves[c][0][:1]
            high_ref[c, pl.ds(j, 1)] = halves[c][1][HALF - 1 :]
        return tuple(pack_edges(list(packed), halves, j, lane))

    packed = lax.fori_loop(
        0, NJ, step, tuple(jnp.zeros((HALF, LANES), F32) for _ in range(COMPS)), unroll=4
    )
    for c in range(COMPS):
        edge_ref[c] = packed[c]
        slab_ref[c] = v_ref[c, 0]
    part_faces(low_ref, high_ref, pair_ref, odd_ref)


def mirror_rows(slab_ref, pair_ref, odd_ref, out_ref):
    even = (lax.axis_index("wrap") & 1) == 0
    for c in range(COMPS):
        pair, odd = pair_ref[c, 0:1], odd_ref[c, 0:1]
        out_ref[c, 0:1] = jnp.where(even, pair, odd)
        for i in range(ROWS):
            out_ref[c, i + 1 : i + 2] = slab_ref[c, ROWS - 1 - i : ROWS - i]
        out_ref[c, ROWS + 1 : ROWS + 2] = jnp.where(even, odd, pair)
        out_ref[c, ROWS + 2 :] = jnp.zeros((24 - ROWS - 2, LANES), F32)


CHUNK = 4
CHUNKS = NJ // CHUNK
AHEAD = 3


def apply_blocks(stage, *refs):
    last = stage == 2
    *refs, even_stage_ref, odd_stage_ref = refs
    (v_ref, slab_ref, jac_ref, src_ref, dis_ref, near_ref, far_face_ref, pair_ref, odd_ref) = refs[:9]
    if stage == 0:
        out_ref, part_ref, low_ref, high_ref, edge_ref, wide_ref, base_ref = refs[9:16]
        q_ref, before_ref, after_ref, narrow_ref, sems = refs[16:]
    elif stage == 1:
        out_ref, part_ref, low_ref, high_ref, edge_ref, q_ref, before_ref, after_ref = refs[9:]
    else:
        far_ref, part_ref, final_ref, q_ref, before_ref, after_ref, out_ref, sems = refs[9:]

    def block_copy(n):
        at = pl.ds(n * CHUNK, CHUNK)
        return pltpu.make_async_copy(
            jac_ref.at[:, :, :, at], narrow_ref.at[:, :, :, at], sems.at[n]
        )

    def result_copy(n):
        at = pl.ds(n * CHUNK, CHUNK)
        return pltpu.make_async_copy(out_ref.at[:, at], far_ref.at[:, at], sems.at[n])

    if stage == 0:
        for n in range(AHEAD):
            block_copy(n).start()
    if last:
        final_copies = (
            pltpu.make_async_copy(v_ref.at[:, 1:NJ], final_ref.at[:, 1:], sems.at[CHUNKS]),
            pltpu.make_async_copy(slab_ref, final_ref.at[:, 0], sems.at[CHUNKS + 1]),
        )
        for copy in final_copies:
            copy.start()
    lane, row = lane_index(), row_index()
    place = lax.axis_index("span")
    has_down, has_up = place > 0, place < SPAN - 1
    swapped = (place & 1) == 1
    part_faces(far_face_ref, near_ref, after_ref, before_ref)
    even = (lane & 1) == 0
    for c in range(COMPS):
        up = jnp.where(swapped, odd_ref[c], pair_ref[c])
        down = jnp.where(swapped, pair_ref[c], odd_ref[c])
        from_up = jnp.where(has_up, pltpu.roll(up, LANES - 1, 1), 0.0)
        from_down = jnp.where(has_down, pltpu.roll(down, 1, 1), 0.0)
        q_ref[c] = jnp.where(even, from_up, from_down)
        if not last:
            out_ref[c, NJ] = jnp.zeros((ROWS, LANES), F32)
    first_lane, last_lane = lane == 0, lane == LANES - 1
    first_row, last_row = row == 0, row == HALF - 1

    def plane(c, j):
        if isinstance(j, int) and j < 0:
            return jnp.zeros((ROWS, LANES), F32)
        return slab_ref[c] if isinstance(j, int) and j == 0 else v_ref[c, j]

    def prepare(j, stage_ref):
        for c in range(COMPS):
            here = plane(c, j)
            a, b = here[:HALF], here[HALF:]
            before = spread(before_ref[c, pl.ds(j, 1)])
            after = spread(after_ref[c, pl.ds(j, 1)])
            a_up, b_up = pltpu.roll(a, HALF - 1, 0), pltpu.roll(b, HALF - 1, 0)
            a_dn, b_dn = pltpu.roll(a, 1, 0), pltpu.roll(b, 1, 0)
            next_i = (jnp.where(last_row, b_up, a_up), jnp.where(last_row, after, b_up))
            prev_i = (jnp.where(first_row, before, a_dn), jnp.where(first_row, a_dn, b_dn))
            for half, x in enumerate((a, b)):
                at = slice(half * HALF, (half + 1) * HALF)
                edge = pltpu.roll(q_ref[c], LANES - 1 - 4 * j - 2 * half, 1)
                next_k = jnp.where(last_lane, edge, pltpu.roll(x, LANES - 1, 1))
                prev_k = jnp.where(first_lane, edge, pltpu.roll(x, 1, 1))
                stage_ref[c, at] = next_i[half] - prev_i[half]
                stage_ref[COMPS + c, at] = next_k - prev_k
                stage_ref[2 * COMPS + c, at] = (next_i[half] + prev_i[half]) + (next_k + prev_k)

    def combine(j, stage_ref):
        total = [None] * COMPS
        sums = [None] * COMPS
        for b in range(COMPS):
            below = plane(b, j - 1)
            if last and isinstance(j, int) and j == NJ - 1:
                above = jnp.zeros((ROWS, LANES), F32)
            else:
                above = plane(b, j + 1)
            sums[b] = stage_ref[2 * COMPS + b] + (above + below)
            for d, diff in ((0, stage_ref[b]), (1, above - below), (2, stage_ref[COMPS + b])):
                for c in range(COMPS):
                    if stage == 0:
                        block = narrow_ref[d, c, b, j].astype(F32)
                        wide_ref[d, c, b, j] = block
                        if d == 1 and isinstance(j, int) and j == 0:
                            base_ref[c, b] = block
                    else:
                        block = jac_ref[d, c, b, j]
                    term = block * diff
                    total[c] = term if total[c] is None else total[c] + term
        dis = dis_ref[j]
        weight = None if last else (OMEGA / 6.0) / dis
        for c in range(COMPS):
            x = plane(c, j)
            rhs = src_ref[c, j] - total[c]
            if last:
                rest = rhs - dis * (6.0 * x - sums[c])
            else:
                rest = ((1.0 - OMEGA) * x + (OMEGA / 6.0) * sums[c]) + weight * rhs
            if isinstance(j, int) and j == 0:
                part_ref[c] = rest
            out_ref[c, j] = rest
            if not last:
                low_ref[c, pl.ds(j, 1)] = rest[:1]
                high_ref[c, pl.ds(j, 1)] = rest[ROWS - 1 :]

    def pack(j, packed):
        if last:
            return packed
        halves = [(out_ref[c, j, :HALF], out_ref[c, j, HALF:]) for c in range(COMPS)]
        return tuple(pack_edges(list(packed), halves, j, lane))

    def loop_step(t, packed):
        j = 2 * t + 2
        if stage == 0:

            @pl.when(j % CHUNK == 0)
            def _():
                n = j // CHUNK
                block_copy(n).wait()

                @pl.when(n + AHEAD < CHUNKS)
                def _():
                    block_copy(n + AHEAD).start()

        packed = pack(j - 1, packed)
        prepare(j + 1, odd_stage_ref)
        combine(j, even_stage_ref)
        packed = pack(j, packed)
        prepare(jnp.minimum(j + 2, NJ - 1), even_stage_ref)
        combine(j + 1, odd_stage_ref)
        if last:

            @pl.when(j % CHUNK == CHUNK - 2)
            def _():
                result_copy(j // CHUNK).start()

        return packed

    packed = () if last else tuple(jnp.zeros((HALF, LANES), F32) for _ in range(COMPS))
    if stage == 0:
        block_copy(0).wait()
        block_copy(AHEAD).start()
    prepare(0, even_stage_ref)
    prepare(1, odd_stage_ref)
    combine(0, even_stage_ref)
    packed = pack(0, packed)
    prepare(2, even_stage_ref)
    combine(1, odd_stage_ref)
    packed = lax.fori_loop(0, NJ // 2 - 1, loop_step, packed)
    packed = pack(NJ - 1, packed)
    if last:
        for n in range(CHUNKS):
            result_copy(n).wait()
        for copy in final_copies:
            copy.wait()
    else:
        for c in range(COMPS):
            edge_ref[c] = packed[c]


def add_ghosts(last, *refs):
    (slab_ref, base_ref, dis_ref, wall_ref, partner_ref, window_ref, part_ref) = refs[:7]
    if last:
        _, far_ref, out_ref, sem = refs[7:]
    else:
        low_in, high_in, edge_in, out_ref, pair_ref, odd_ref, edge_ref = refs[7:]
        part_faces(low_in, high_in, pair_ref, odd_ref)
        even = (lax.axis_index("wrap") & 1) == 0
    lane = lane_index()
    base = lax.axis_index("wrap") * ROWS
    row = lax.broadcasted_iota(jnp.int32, (ROWS, LANES), 0)
    shift = partner_ref[...] - (WRAP * ROWS - 1 - base - row)
    wall = wall_ref[...] == 1
    dis = dis_ref[0]
    ghosts = []
    for c in range(COMPS):
        rows = window_ref[c]
        lower, middle, upper = rows[:ROWS], rows[1 : ROWS + 1], rows[2 : ROWS + 2]
        chosen = jnp.where(shift == -1, upper, jnp.where(shift == 1, lower, middle))
        ghosts.append(jnp.where(wall, slab_ref[c], chosen))
    if not last:
        weight = (OMEGA / 6.0) / dis
    for c in range(COMPS):
        total = base_ref[c, 0] * ghosts[0]
        for b in range(1, COMPS):
            total = total + base_ref[c, b] * ghosts[b]
        if last:
            fresh = part_ref[c] + (dis * ghosts[c] + total)
        else:
            fresh = part_ref[c] + ((OMEGA / 6.0) * ghosts[c] + weight * total)
        out_ref[c] = fresh
        if not last:
            low, high = fresh[:1], fresh[ROWS - 1 :]
            pair_ref[c, 0:1] = jnp.where(even, high, low)
            odd_ref[c, 0:1] = jnp.where(even, low, high)
            edge = jnp.where(lane < 2, pltpu.roll(fresh[:HALF], 1, 1), edge_in[c])
            here = (lane == 2) | (lane == 3)
            edge_ref[c] = jnp.where(here, pltpu.roll(fresh[HALF:], 3, 1), edge)
    if last:
        copy = pltpu.make_async_copy(out_ref, far_ref.at[:, 0], sem)
        copy.start()
        copy.wait()


POINT_LANES = 64


def surface_sums(*refs):
    slab_ref, slope_ref, wall_ref, points_ref, weights_ref, face_ref = refs[:6]
    kept_ref, bundle_ref, left_ref, right_ref, sum_ref = refs[6:]
    bundle_ref[:COMPS] = face_ref[...]
    wall = wall_ref[...].astype(F32)
    grads = []
    for x in range(3):
        total = slope_ref[x, 0] * slab_ref[0]
        for a in range(1, COMPS):
            total = total + slope_ref[x, a] * slab_ref[a]
        grads.append(total * wall)
    owner = lax.broadcasted_iota(jnp.int32, (WRAP, LANES), 0)
    inner = lax.broadcasted_iota(jnp.int32, (POINT_LANES, LANES), 0)
    for slot in range(LISTS):
        points = points_ref[slot]
        scale = weights_ref[slot]
        major, minor = points >> 6, points & (POINT_LANES - 1)
        parts = []
        for x in range(3):
            value = grads[x] * scale
            high = value.astype(BF16).astype(F32)
            parts.append((high, value - high))
        for i in range(ROWS):
            at = pl.ds((slot * ROWS + i) * LANES, LANES)
            mine = owner == jnp.broadcast_to(major[i : i + 1], (WRAP, LANES))
            for x in range(3):
                for part in range(2):
                    value = jnp.broadcast_to(parts[x][part][i : i + 1], (WRAP, LANES))
                    left_ref[x * 2 + part, :, at] = jnp.where(mine, value, 0.0).astype(BF16)
            same = inner == jnp.broadcast_to(minor[i : i + 1], (POINT_LANES, LANES))
            right_ref[:, at] = jnp.where(same, 1.0, 0.0).astype(BF16)
    left = left_ref[...].reshape(6 * WRAP, LISTS * ROWS * LANES)
    product = lax.dot_general(
        left, right_ref[...], (((1,), (1,)), ((), ())), preferred_element_type=F32
    )
    sum_ref[...] = jnp.zeros_like(sum_ref)
    for x in range(3):
        first = product[2 * x * WRAP : (2 * x + 1) * WRAP]
        second = product[(2 * x + 1) * WRAP : (2 * x + 2) * WRAP]
        both = first + second
        for w in range(WRAP):
            place = (w & 9) | ((w ^ (w >> 1)) & 2) | (w & 4)
            sum_ref[place, x : x + 1, :POINT_LANES] = both[w : w + 1]
    mine = lax.axis_index("wrap") & 1
    for n in range(WRAP // 2):
        kept_ref[n] = sum_ref[2 * n + mine]
        bundle_ref[COMPS + n // 4, pl.ds(n % 4 * HALF, HALF)] = sum_ref[2 * n + 1 - mine]


def halve_bundle(kept_in, bundle_ref, kept_ref, sent_ref, sum_ref):
    for n in range(WRAP // 2):
        sum_ref[n] = kept_in[n] + bundle_ref[COMPS + n // 4, n % 4 * HALF : (n % 4 + 1) * HALF]
    w = lax.axis_index("wrap")
    deal(((w >> 1) ^ (w >> 2)) & 1, sum_ref, kept_ref, sent_ref)


def halve(kept_in, got_ref, kept_ref, sent_ref, sum_ref):
    sum_ref[...] = kept_in[...] + got_ref[...]
    deal((lax.axis_index("wrap") >> 2) & 1, sum_ref, kept_ref, sent_ref)


def deal(mine, sum_ref, kept_ref, sent_ref):
    for n in range(kept_ref.shape[0]):
        kept_ref[n] = sum_ref[2 * n + mine]
        sent_ref[n] = sum_ref[2 * n + 1 - mine]


def halve_lanes(kept_in, got_ref, kept_ref, sent_ref):
    first, second = kept_in[0] + got_ref[0], kept_in[1] + got_ref[1]
    mine = (lax.axis_index("wrap") >> 3) ^ (lax.axis_index("span") & 1)
    odd = (lane_index() >> 3) & 1
    take = odd == mine
    kept_ref[0] = jnp.where(take, first, second)
    sent_ref[0] = jnp.where(take, second, first)


def add_tiles(a_ref, b_ref, out_ref):
    out_ref[...] = a_ref[...] + b_ref[...]


def finish_points(a_ref, b_ref, out_ref):
    total = a_ref[0] + b_ref[0]
    out_ref[...] = pltpu.roll(total, LANES - 8 * lax.axis_index("span"), 1)[:3, :8]


def masked(wrap_mask, span_mask):
    return [
        (w * SPAN + s, (w ^ wrap_mask) * SPAN + (s ^ span_mask))
        for w in range(WRAP)
        for s in range(SPAN)
    ]


FOLDS = (masked(2, 0), masked(6, 0), masked(8, 0), masked(8, 1), masked(0, 2), masked(0, 6))


def fold(x, n):
    return lax.ppermute(x, ("wrap", "span"), FOLDS[n - 1])


def reduce_points(kept, bundle):
    tiles = lambda n: [shape_of(n, HALF, LANES)]
    room = lambda n: (pltpu.VMEM((n, HALF, LANES), F32),)
    kept, sent = run_kernel(halve_bundle, tiles(4) * 2, (kept, bundle), scratch=room(8))
    args = (kept, fold(sent, 1))
    kept, sent = run_kernel(halve, tiles(2) * 2, args, scratch=room(4))
    args = (kept, fold(sent, 2))
    kept, sent = run_kernel(halve_lanes, tiles(1) * 2, args)
    got = fold(sent, 3)
    for n in range(4, 7):
        (kept,) = run_kernel(add_tiles, tiles(1), (kept, got))
        got = fold(kept, n)
    (out,) = run_kernel(finish_points, [shape_of(3, 8)], (kept, got))
    return out


WRAP_PAIR = [(i, i ^ 1) for i in range(WRAP)]
WRAP_ODD = [(i, (i + 1) % WRAP if i % 2 else (i - 1) % WRAP) for i in range(WRAP)]
SPAN_PAIR = [(i, i ^ 1) for i in range(SPAN)]
SPAN_ODD = [(i, (i + 1) % SPAN if i % 2 else (i - 1) % SPAN) for i in range(SPAN)]
MIRROR = [(i, WRAP - 1 - i) for i in range(WRAP)]

FIELD = (COMPS, NJ, ROWS, LANES)
TALL = (COMPS, NJ + 1, ROWS, LANES)
SLAB = (COMPS, ROWS, LANES)
STAGE = (3 * COMPS, ROWS, LANES)
FACE = (COMPS, NJ, LANES)
EDGE = (COMPS, HALF, LANES)
BLOCKS = (3, COMPS, COMPS, NJ, ROWS, LANES)
SWEEP_FLOPS = 160 * COMPS * NJ * ROWS * LANES
DMA = pltpu.SemaphoreType.DMA


def exchange(slab, pair_face, odd_face, edge):
    near = lax.ppermute(pair_face, "wrap", WRAP_PAIR)
    far = lax.ppermute(odd_face, "wrap", WRAP_ODD)
    odd = lax.ppermute(edge, "span", SPAN_ODD)
    pair = lax.ppermute(edge, "span", SPAN_PAIR)
    (rows,) = run_kernel(mirror_rows, [shape_of(COMPS, 24, LANES)], (slab, near, far))
    window = lax.ppermute(rows, "wrap", MIRROR)
    return (near, far, pair, odd), window


def operator_step(stage, v, slab, faces, blocks, base, fixed):
    source, dissipation, wall, partner = fixed
    halos, window = exchange(slab, *faces)
    args = (v, slab, blocks, source, dissipation, *halos)
    kernel = functools.partial(apply_blocks, stage)
    if stage < 2:
        outs = [shape_of(*d) for d in (TALL, SLAB, FACE, FACE, EDGE)]
        scratch = [pltpu.VMEM(EDGE, F32), pltpu.VMEM(FACE, F32), pltpu.VMEM(FACE, F32)]
        if stage == 0:
            outs += [shape_of(*BLOCKS), shape_of(*BLOCKS[1:3], ROWS, LANES)]
            scratch += [pltpu.VMEM(BLOCKS, BF16), DMA((CHUNKS,))]
        scratch += [pltpu.VMEM(STAGE, F32)] * 2
        v, part, *rest = run_kernel(
            kernel,
            outs,
            args,
            scratch=scratch,
            flops=SWEEP_FLOPS,
            far=(2,) if stage == 0 else (),
            vmem=12 if stage == 0 else 4,
        )
        if stage == 0:
            *rest, blocks, base = rest
        slab, *faces = run_kernel(
            functools.partial(add_ghosts, False),
            [shape_of(*d) for d in (SLAB, FACE, FACE, EDGE)],
            (slab, base, dissipation, wall, partner, window, part, *rest),
            flops=1000000,
        )
        return v, slab, faces, blocks, base
    residual, part, final = run_kernel(
        kernel,
        [shape_of(*FIELD), shape_of(*SLAB), shape_of(*FIELD)],
        args,
        scratch=(
            pltpu.VMEM(EDGE, F32),
            pltpu.VMEM(FACE, F32),
            pltpu.VMEM(FACE, F32),
            pltpu.VMEM(FIELD, F32),
            DMA((CHUNKS + 2,)),
            pltpu.VMEM(STAGE, F32),
            pltpu.VMEM(STAGE, F32),
        ),
        flops=SWEEP_FLOPS,
        far_out=(0, 2),
    )
    (residual,) = run_kernel(
        functools.partial(add_ghosts, True),
        [shape_of(*FIELD)],
        (slab, base, dissipation, wall, partner, window, part, residual),
        scratch=(pltpu.VMEM(SLAB, F32), DMA),
        aliases={7: 0},
        flops=1000000,
        far=(7,),
        far_out=(0,),
    )
    return final, residual, halos[0]


def program(
    adjoint_start,
    adjoint_source,
    jacobians,
    dissipation,
    wall_mask,
    wake_partner,
    surface_slopes,
    control_points,
    control_weights,
):
    fixed = (adjoint_source, dissipation, wall_mask, wake_partner)
    v, slab, *faces = run_kernel(
        first_faces,
        [shape_of(*d) for d in (TALL, SLAB, FACE, FACE, EDGE)],
        (pltpu.with_memory_space_constraint(adjoint_start, pltpu.HBM),),
        scratch=(pltpu.VMEM(FACE, F32), pltpu.VMEM(FACE, F32), DMA),
        flops=1000000,
        far=(0,),
    )
    blocks, base = pltpu.with_memory_space_constraint(jacobians, pltpu.HBM), None
    for stage in range(2):
        v, slab, faces, blocks, base = operator_step(
            stage, v, slab, faces, blocks, base, fixed
        )
    kept, bundle = run_kernel(
        surface_sums,
        [shape_of(WRAP // 2, HALF, LANES), shape_of(COMPS + 2, NJ, LANES)],
        (slab, surface_slopes, wall_mask, control_points, control_weights, faces[0]),
        scratch=(
            pltpu.VMEM((6, WRAP, LISTS * ROWS * LANES), BF16),
            pltpu.VMEM((POINT_LANES, LISTS * ROWS * LANES), BF16),
            pltpu.VMEM((WRAP, HALF, LANES), F32),
        ),
        flops=10000000,
        vmem=8,
    )
    faces[0] = bundle
    final, residual, bundle = operator_step(2, v, slab, faces, blocks, base, fixed)
    shape_gradient = reduce_points(kept, bundle)
    return final, residual, shape_gradient


def solution(mesh):
    in_specs = (
        P(None, None, "wrap", "span"),
        P(None, None, "wrap", "span"),
        P(None, None, None, None, "wrap", "span"),
        P(None, "wrap", "span"),
        P("wrap", "span"),
        P("wrap", "span"),
        P(None, None, "wrap", "span"),
        P(None, "wrap", "span"),
        P(None, "wrap", "span"),
    )
    out_specs = (
        P(None, None, "wrap", "span"),
        P(None, None, "wrap", "span"),
        P(None, ("wrap", "span")),
    )
    return jax.shard_map(program, mesh=mesh, in_specs=in_specs, out_specs=out_specs, check_vma=False)
```

time: 97.6 us -> 86.3 us (0.88)
  starting transfers between devices: 48.2 us -> 29.3 us
  waiting for transfers between devices: 24.8 us -> 37.2 us
  Pallas kernels: 23.6 us -> 18.8 us
    ppermute x19 -> x18, starting transfers between devices: 35.9 us -> 22.8 us  [the longest x3 11.2 us: exchange(): odd = lax.ppermute(edge, 'span', SPAN_ODD)]
    ppermute x19 -> x18, waiting for transfers between devices: 24.8 us -> 37.2 us  [the longest x6 14.9 us: fold(): return lax.ppermute(x, ('wrap', 'span'), FOLDS[n - 1])]
    ppermute x3, starting transfers between devices: 12.3 us -> 6.5 us  [exchange(): window = lax.ppermute(rows, 'wrap', MIRROR)]
    pallas_call x18, Pallas kernels: 23.6 us -> 18.8 us  [run_kernel(): pl.pallas_call(kernel, out_shape=outs, in_specs=[FARSPEC if n in far else...]
  transfers between devices with their start and end apart: 22 -> 21, of which waited for: 12 -> 13; matrix products, arithmetic and copies ran while one was open for 0% -> 0% of each run, Pallas kernels for 21% -> 17%
where the time goes in v1:
time: 86.3 us; the launch traced here: 86.2 us
  waiting for transfers between devices  37.2 us (43%)
  starting transfers between devices  29.3 us (34%)
  Pallas kernels  18.8 us (22%)
    pallas_call x18, Pallas kernels, run_kernel(): pl.pallas_call(kernel, out_shape=outs, in_specs=[FARSPEC if n in far else...  18.8 us
    ppermute x6, waiting for transfers between devices, fold(): return lax.ppermute(x, ('wrap', 'span'), FOLDS[n - 1])  14.9 us
    ppermute x3, starting transfers between devices, exchange(): odd = lax.ppermute(edge, 'span', SPAN_ODD)  11.2 us
    ppermute x3, waiting for transfers between devices, exchange(): far = lax.ppermute(odd_face, 'wrap', WRAP_ODD)  10.5 us
    ppermute x3, starting transfers between devices, exchange(): far = lax.ppermute(odd_face, 'wrap', WRAP_ODD)  7.83 us
    ppermute x3, waiting for transfers between devices, exchange(): odd = lax.ppermute(edge, 'span', SPAN_ODD)  7.48 us
    ppermute x3, starting transfers between devices, exchange(): window = lax.ppermute(rows, 'wrap', MIRROR)  6.5 us
    ppermute x6, starting transfers between devices, fold(): return lax.ppermute(x, ('wrap', 'span'), FOLDS[n - 1])  3.41 us
  transfers between devices with their start and end apart: 21, of which 13 were waited for; matrix products, arithmetic and copies ran while one was open for 0% of the time, Pallas kernels for 17%

profile of v1, /device:TPU:0, one launch (start us, length us, event | category | flops | bytes accessed | tf_op | source)
XLA Modules:
  0.0 86.2 jit_solution(10807492357767195936)
XLA Ops:
  0.7 2.4 %shard_map.112 = (f32[5,33,16,128]{3,2,1,0:T(8,128)S(1)}, f32[5,16,128]{2,1,0:T(8,128)S(1)}, f32[5,32,128]{2,1,0:T(8,128)S(1)}, f32[5,32,128]{2,1,0:T(8,128)S(1)}, f32[5,8,128]{2,1,0:T(8,128)S(1)}) custom-call(f32[5,32,16,128]{3,2,1,0:T(8,128)} %start_ref.1), custom_call_target="tpu_custom_call" | custom-call | flops 1000000 | bytes 1310720 | tf_op jit(solution)/shard_map/pallas_call | solution.py:33
  3.0 0.1 collective-permute-start
  3.1 5.3 %collective-permute-start.1 = (f32[5,32,128]{2,1,0:T(8,128)S(1)}, f32[5,32,128]{2,1,0:T(8,128)S(1)}, u32[]{:S(2)}, u32[]{:S(2)}) collective-permute-start(f32[5,32,128]{2,1,0:T(8,128)S(1)} %get-tuple-element.42), channel_id=1, source_target_pairs={{0,120},{8,16},{16,8},{24,32},{32,24},{40,48},{48,40},{56,64},{64,... | collective-permute-start | bytes 245768 | tf_op jit(solution)/shard_map/ppermute | solution.py:460
  8.4 0.0 collective-permute-done.refs_5_.pair_ref
  8.4 2.1 %collective-permute-done.1.refs_6_.odd_ref = f32[5,32,128]{2,1,0:T(8,128)S(1)} collective-permute-done((f32[5,32,128]{2,1,0:T(8,128)S(1)}, f32[5,32,128]{2,1,0:T(8,128)S(1)}, u32[]{:S(2)}, u32[]{:S(2)}) %collective-permute-start.1) | collective-permute-done | bytes 81952 | tf_op jit(solution)/shard_map/ppermute | solution.py:460
  10.6 3.9 %collective-permute-start.4 = (f32[5,24,128]{2,1,0:T(8,128)S(1)}, f32[5,24,128]{2,1,0:T(8,128)S(1)}, u32[]{:S(2)}, u32[]{:S(2)}) collective-permute-start(f32[5,24,128]{2,1,0:T(8,128)S(1)} %shard_map.114), channel_id=1, source_target_pairs={{0,120},{8,112},{16,104},{24,96},{32,88},{40,80},{48,72},{56,64},{... | collective-permute-start | bytes 184328 | tf_op jit(solution)/shard_map/ppermute | solution.py:464
  14.5 5.1 %collective-permute-start.3 = (f32[5,8,128]{2,1,0:T(8,128)S(1)}, f32[5,8,128]{2,1,0:T(8,128)S(1)}, u32[]{:S(2)}, u32[]{:S(2)}) collective-permute-start(f32[5,8,128]{2,1,0:T(8,128)S(1)} %get-tuple-element.43), channel_id=1, source_target_pairs={{0,7},{1,2},{2,1},{3,4},{4,3},{5,6},{6,5},{7,0},{8,15},{9,10},{10,... | collective-permute-start | bytes 61448 | tf_op jit(solution)/shard_map/ppermute | solution.py:461
  19.6 0.0 collective-permute-start.2
  19.6 2.3 %collective-permute-done.3.refs_8_ = f32[5,8,128]{2,1,0:T(8,128)S(1)} collective-permute-done((f32[5,8,128]{2,1,0:T(8,128)S(1)}, f32[5,8,128]{2,1,0:T(8,128)S(1)}, u32[]{:S(2)}, u32[]{:S(2)}) %collective-permute-start.3) | collective-permute-done | bytes 20512 | tf_op jit(solution)/shard_map/ppermute | solution.py:461
  21.9 3.0 %collective-permute-done.2.refs_7_ = f32[5,8,128]{2,1,0:T(8,128)S(1)} collective-permute-done((f32[5,8,128]{2,1,0:T(8,128)S(1)}, f32[5,8,128]{2,1,0:T(8,128)S(1)}, u32[]{:S(2)}, u32[]{:S(2)}) %collective-permute-start.2) | collective-permute-done | bytes 20512 | tf_op jit(solution)/shard_map/ppermute | solution.py:462
  24.9 5.6 %shard_map.113 = (f32[5,33,16,128]{3,2,1,0:T(8,128)S(1)}, f32[5,16,128]{2,1,0:T(8,128)S(1)}, f32[5,32,128]{2,1,0:T(8,128)S(1)}, f32[5,32,128]{2,1,0:T(8,128)S(1)...) custom-call(f32[5,33,16,128]{3,2,1,0:T(8,128)S(1)} %get-tuple-element.39.refs_0_, ...), custom_call_target="tpu_custom_call" | custom-call | flops 52428800 | bytes 13000704 | tf_op jit(solution)/shard_map/pallas_call | solution.py:33
  30.5 0.0 collective-permute-done.4.refs_5_
  30.6 0.1 shard_map.115
  30.7 0.1 collective-permute-start.5
  30.8 0.1 collective-permute-start.6
  30.9 1.2 %collective-permute-done.5.refs_5_.pair_ref = f32[5,32,128]{2,1,0:T(8,128)S(1)} collective-permute-done((f32[5,32,128]{2,1,0:T(8,128)S(1)}, f32[5,32,128]{2,1,0:T(8,128)S(1)}, u32[]{:S(2)}, u32[]{:S(2)}) %collective-permute-start.5) | collective-permute-done | bytes 81952 | tf_op jit(solution)/shard_map/ppermute | solution.py:459
  32.0 4.8 %collective-permute-done.6.refs_6_.odd_ref = f32[5,32,128]{2,1,0:T(8,128)S(1)} collective-permute-done((f32[5,32,128]{2,1,0:T(8,128)S(1)}, f32[5,32,128]{2,1,0:T(8,128)S(1)}, u32[]{:S(2)}, u32[]{:S(2)}) %collective-permute-start.6) | collective-permute-done | bytes 81952 | tf_op jit(solution)/shard_map/ppermute | solution.py:460
  36.9 0.1 collective-permute-start.9
  37.0 2.2 %collective-permute-start.8 = (f32[5,8,128]{2,1,0:T(8,128)S(1)}, f32[5,8,128]{2,1,0:T(8,128)S(1)}, u32[]{:S(2)}, u32[]{:S(2)}) collective-permute-start(f32[5,8,128]{2,1,0:T(8,128)S(1)} %get-tuple-element.54), channel_id=1, source_target_pairs={{0,7},{1,2},{2,1},{3,4},{4,3},{5,6},{6,5},{7,0},{8,15},{9,10},{10,... | collective-permute-start | bytes 61448 | tf_op jit(solution)/shard_map/ppermute | solution.py:461
  39.2 0.1 collective-permute-start.7
  39.3 5.2 %collective-permute-done.8.refs_8_ = f32[5,8,128]{2,1,0:T(8,128)S(1)} collective-permute-done((f32[5,8,128]{2,1,0:T(8,128)S(1)}, f32[5,8,128]{2,1,0:T(8,128)S(1)}, u32[]{:S(2)}, u32[]{:S(2)}) %collective-permute-start.8) | collective-permute-done | bytes 20512 | tf_op jit(solution)/shard_map/ppermute | solution.py:461
  44.5 0.2 collective-permute-done.7.refs_7_
  44.7 3.8 %shard_map.116 = (f32[5,33,16,128]{3,2,1,0:T(8,128)S(1)}, f32[5,16,128]{2,1,0:T(8,128)S(1)}, f32[5,32,128]{2,1,0:T(8,128)S(1)}, f32[5,32,128]{2,1,0:T(8,128)S(1)}, f32[5,8,128]{2,1,0:T(8,128)S(1)}) custom-call(f32[5,33,16,128]{3,2,1,0:T(8,128)S(1)} %get-tuple-element.44.refs_0_, f32[5,16,128]{2,1,0:T(8,128)S(1)} %get-tuple-element.50.refs_1_.slab_ref.refs_0_, ...), custom_call_target="tpu_custom_call" | custom-call | flops 52428800 | bytes 22831104 | tf_op jit(solution)/shard_map/pallas_call | solution.py:33
  48.5 0.0 collective-permute-done.9.refs_5_
  48.5 0.1 shard_map.118
  48.7 1.1 %shard_map.119 = (f32[8,8,128]{2,1,0:T(8,128)S(1)}, f32[7,32,128]{2,1,0:T(8,128)S(1)}) custom-call(f32[5,16,128]{2,1,0:T(8,128)S(1)} %get-tuple-element.60.refs_0_.refs_1_.slab_ref, f32[3,5,16,128]{3,2,1,0:T(8,128)S(1)} %copy-done.3, s32[16,128]{1,0:T(8,128)S(1)} %copy-done.2, s32[4,16,128]{2,1,0:T(8,128)S(1)} %copy-done.5, f32[4,16,128]{2,1,0:T(8,128)S(1)} %copy-done.6, ...), custom_call_target="tpu_custom_call" | custom-call | flops 10000000 | bytes 319488 | tf_op jit(solution)/shard_map/pallas_call | solution.py:33
  49.8 0.1 collective-permute-start.10
  49.9 2.5 %collective-permute-start.11 = (f32[5,32,128]{2,1,0:T(8,128)S(1)}, f32[5,32,128]{2,1,0:T(8,128)S(1)}, u32[]{:S(2)}, u32[]{:S(2)}) collective-permute-start(f32[5,32,128]{2,1,0:T(8,128)S(1)} %get-tuple-element.63), channel_id=1, source_target_pairs={{0,120},{8,16},{16,8},{24,32},{32,24},{40,48},{48,40},{56,64},{64,... | collective-permute-start | bytes 245768 | tf_op jit(solution)/shard_map/ppermute | solution.py:460
  52.4 3.6 %collective-permute-done.11.refs_6_.odd_ref = f32[5,32,128]{2,1,0:T(8,128)S(1)} collective-permute-done((f32[5,32,128]{2,1,0:T(8,128)S(1)}, f32[5,32,128]{2,1,0:T(8,128)S(1)}, u32[]{:S(2)}, u32[]{:S(2)}) %collective-permute-start.11) | collective-permute-done | bytes 81952 | tf_op jit(solution)/shard_map/ppermute | solution.py:460
  55.9 0.0 collective-permute-done.10.refs_5_.pair_ref.bundle_ref
  56.0 2.5 %collective-permute-start.14 = (f32[5,24,128]{2,1,0:T(8,128)S(1)}, f32[5,24,128]{2,1,0:T(8,128)S(1)}, u32[]{:S(2)}, u32[]{:S(2)}) collective-permute-start(f32[5,24,128]{2,1,0:T(8,128)S(1)} %shard_map.121), channel_id=1, source_target_pairs={{0,120},{8,112},{16,104},{24,96},{32,88},{40,80},{48,72},{56,64},{... | collective-permute-start | bytes 184328 | tf_op jit(solution)/shard_map/ppermute | solution.py:464
  58.5 0.1 collective-permute-start.15
  58.6 3.7 %collective-permute-done.15.got_ref = f32[4,8,128]{2,1,0:T(8,128)S(1)} collective-permute-done((f32[4,8,128]{2,1,0:T(8,128)S(1)}, f32[4,8,128]{2,1,0:T(8,128)S(1)}, u32[]{:S(2)}, u32[]{:S(2)}) %collective-permute-start.15) | collective-permute-done | bytes 16416 | tf_op jit(solution)/shard_map/ppermute | solution.py:422
  62.3 3.9 %collective-permute-start.13 = (f32[5,8,128]{2,1,0:T(8,128)S(1)}, f32[5,8,128]{2,1,0:T(8,128)S(1)}, u32[]{:S(2)}, u32[]{:S(2)}) collective-permute-start(f32[5,8,128]{2,1,0:T(8,128)S(1)} %get-tuple-element.64), channel_id=1, source_target_pairs={{0,7},{1,2},{2,1},{3,4},{4,3},{5,6},{6,5},{7,0},{8,15},{9,10},{10,... | collective-permute-start | bytes 61448 | tf_op jit(solution)/shard_map/ppermute | solution.py:461
  66.2 0.9 %collective-permute-done.16.got_ref = f32[2,8,128]{2,1,0:T(8,128)S(1)} collective-permute-done((f32[2,8,128]{2,1,0:T(8,128)S(1)}, f32[2,8,128]{2,1,0:T(8,128)S(1)}, u32[]{:S(2)}, u32[]{:S(2)}) %collective-permute-start.16) | collective-permute-done | bytes 8224 | tf_op jit(solution)/shard_map/ppermute | solution.py:422
  67.2 0.5 collective-permute-start.17
  67.7 3.1 %collective-permute-done.17.b_ref = f32[1,8,128]{2,1,0:T(8,128)S(1)} collective-permute-done((f32[1,8,128]{2,1,0:T(8,128)S(1)}, f32[1,8,128]{2,1,0:T(8,128)S(1)}, u32[]{:S(2)}, u32[]{:S(2)}) %collective-permute-start.17) | collective-permute-done | bytes 4128 | tf_op jit(solution)/shard_map/ppermute | solution.py:422
  70.8 1.3 %collective-permute-start.18 = (f32[1,8,128]{2,1,0:T(8,128)S(1)}, f32[1,8,128]{2,1,0:T(8,128)S(1)}, u32[]{:S(2)}, u32[]{:S(2)}) collective-permute-start(f32[1,8,128]{2,1,0:T(8,128)S(1)} %shard_map.126.a_ref), channel_id=1, source_target_pairs={{0,65},{1,64},{2,67},{3,66},{4,69},{5,68},{6,71},{7,70},{8,73},{9,... | collective-permute-start | bytes 12296 | tf_op jit(solution)/shard_map/ppermute | solution.py:422
  72.1 3.5 %collective-permute-done.18.b_ref = f32[1,8,128]{2,1,0:T(8,128)S(1)} collective-permute-done((f32[1,8,128]{2,1,0:T(8,128)S(1)}, f32[1,8,128]{2,1,0:T(8,128)S(1)}, u32[]{:S(2)}, u32[]{:S(2)}) %collective-permute-start.18) | collective-permute-done | bytes 4128 | tf_op jit(solution)/shard_map/ppermute | solution.py:422
  75.6 0.0 collective-permute-start.19
  75.6 3.6 %collective-permute-done.19.b_ref = f32[1,8,128]{2,1,0:T(8,128)S(1)} collective-permute-done((f32[1,8,128]{2,1,0:T(8,128)S(1)}, f32[1,8,128]{2,1,0:T(8,128)S(1)}, u32[]{:S(2)}, u32[]{:S(2)}) %collective-permute-start.19) | collective-permute-done | bytes 4128 | tf_op jit(solution)/shard_map/ppermute | solution.py:422
  79.2 1.5 %collective-permute-start.20 = (f32[1,8,128]{2,1,0:T(8,128)S(1)}, f32[1,8,128]{2,1,0:T(8,128)S(1)}, u32[]{:S(2)}, u32[]{:S(2)}) collective-permute-start(f32[1,8,128]{2,1,0:T(8,128)S(1)} %shard_map.128.a_ref), channel_id=1, source_target_pairs={{0,6},{1,7},{2,4},{3,5},{4,2},{5,3},{6,0},{7,1},{8,14},{9,15},{10,... | collective-permute-start | bytes 12296 | tf_op jit(solution)/shard_map/ppermute | solution.py:422
  80.7 0.0 collective-permute-done.13.refs_8_
  80.7 0.0 collective-permute-done.12.refs_7_
  80.8 4.1 %shard_map.120 = (f32[5,32,16,128]{3,2,1,0:T(8,128)}, f32[5,16,128]{2,1,0:T(8,128)S(1)}, f32[5,32,16,128]{3,2,1,0:T(8,128)}) custom-call(f32[5,33,16,128]{3,2,1,0:T(8,128)S(1)} %get-tuple-element.55.refs_0_, f32[5,16,128]{2,1,0:T(8,128)S(1)} %get-tuple-element.60.refs_0_.refs_1_.slab_ref, f32[3,5,5,32,16,128]{5,4,3,2,1,0:T(8,128)S(1)} %get-tuple-element.51.refs_2_, ...), custom_call_target="tpu_custom_call" | custom-call | flops 52428800 | bytes 22863872 | tf_op jit(solution)/shard_map/pallas_call | solution.py:33
  84.8 0.7 shard_map.129
  85.5 0.0 collective-permute-done.14.refs_5_
  85.5 0.7 shard_map.122
  (26 shorter events, 0.2 us)
Async XLA Ops:
  0.6 24.3 %copy-start.1 = (f32[32,16,128]{2,1,0:T(8,128)S(1)}, f32[32,16,128]{2,1,0:T(8,128)}, u32[]{:S(2)}) copy-start(f32[32,16,128]{2,1,0:T(8,128)} %refs_2_.9) | copy-start | bytes 786436
  0.6 24.2 %copy-start = (f32[5,32,16,128]{3,2,1,0:T(8,128)S(1)}, f32[5,32,16,128]{3,2,1,0:T(8,128)}, u32[]{:S(2)}) copy-start(f32[5,32,16,128]{3,2,1,0:T(8,128)} %refs_3_.12) | copy-start | bytes 3932164
  3.0 5.4 %collective-permute-start = (f32[5,32,128]{2,1,0:T(8,128)S(1)}, f32[5,32,128]{2,1,0:T(8,128)S(1)}, u32[]{:S(2)}, u32[]{:S(2)}) collective-permute-start(f32[5,32,128]{2,1,0:T(8,128)S(1)} %get-tuple-element.41), channel_id=1, source_target_pairs={{0,8},{8,0},{16,24},{24,16},{32,40},{40,32},{48,56},{56,48},{64,72... | collective-permute-start | bytes 245768 | tf_op jit(solution)/shard_map/ppermute | solution.py:459
  3.1 7.4 %collective-permute-start.1 = (f32[5,32,128]{2,1,0:T(8,128)S(1)}, f32[5,32,128]{2,1,0:T(8,128)S(1)}, u32[]{:S(2)}, u32[]{:S(2)}) collective-permute-start(f32[5,32,128]{2,1,0:T(8,128)S(1)} %get-tuple-element.42), channel_id=1, source_target_pairs={{0,120},{8,16},{16,8},{24,32},{32,24},{40,48},{48,40},{56,64},{64,... | collective-permute-start | bytes 245768 | tf_op jit(solution)/shard_map/ppermute | solution.py:460
  10.6 20.0 %collective-permute-start.4 = (f32[5,24,128]{2,1,0:T(8,128)S(1)}, f32[5,24,128]{2,1,0:T(8,128)S(1)}, u32[]{:S(2)}, u32[]{:S(2)}) collective-permute-start(f32[5,24,128]{2,1,0:T(8,128)S(1)} %shard_map.114), channel_id=1, source_target_pairs={{0,120},{8,112},{16,104},{24,96},{32,88},{40,80},{48,72},{56,64},{... | collective-permute-start | bytes 184328 | tf_op jit(solution)/shard_map/ppermute | solution.py:464
  14.5 7.4 %collective-permute-start.3 = (f32[5,8,128]{2,1,0:T(8,128)S(1)}, f32[5,8,128]{2,1,0:T(8,128)S(1)}, u32[]{:S(2)}, u32[]{:S(2)}) collective-permute-start(f32[5,8,128]{2,1,0:T(8,128)S(1)} %get-tuple-element.43), channel_id=1, source_target_pairs={{0,7},{1,2},{2,1},{3,4},{4,3},{5,6},{6,5},{7,0},{8,15},{9,10},{10,... | collective-permute-start | bytes 61448 | tf_op jit(solution)/shard_map/ppermute | solution.py:461
  19.6 5.3 %collective-permute-start.2 = (f32[5,8,128]{2,1,0:T(8,128)S(1)}, f32[5,8,128]{2,1,0:T(8,128)S(1)}, u32[]{:S(2)}, u32[]{:S(2)}) collective-permute-start(f32[5,8,128]{2,1,0:T(8,128)S(1)} %get-tuple-element.43), channel_id=1, source_target_pairs={{0,1},{1,0},{2,3},{3,2},{4,5},{5,4},{6,7},{7,6},{8,9},{9,8},{10,11... | collective-permute-start | bytes 61448 | tf_op jit(solution)/shard_map/ppermute | solution.py:462
  24.9 5.7 %copy-start.2 = (s32[16,128]{1,0:T(8,128)S(1)}, s32[16,128]{1,0:T(8,128)}, u32[]{:S(2)}) copy-start(s32[16,128]{1,0:T(8,128)} %refs_3_.13) | copy-start | bytes 24580
  24.9 5.7 %copy-start.4 = (s32[16,128]{1,0:T(8,128)S(1)}, s32[16,128]{1,0:T(8,128)}, u32[]{:S(2)}) copy-start(s32[16,128]{1,0:T(8,128)} %refs_4_.13) | copy-start | bytes 24580
  30.7 1.3 %collective-permute-start.5 = (f32[5,32,128]{2,1,0:T(8,128)S(1)}, f32[5,32,128]{2,1,0:T(8,128)S(1)}, u32[]{:S(2)}, u32[]{:S(2)}) collective-permute-start(f32[5,32,128]{2,1,0:T(8,128)S(1)} %get-tuple-element.52), channel_id=1, source_target_pairs={{0,8},{8,0},{16,24},{24,16},{32,40},{40,32},{48,56},{56,48},{64,72... | collective-permute-start | bytes 245768 | tf_op jit(solution)/shard_map/ppermute | solution.py:459
  30.8 6.1 %collective-permute-start.6 = (f32[5,32,128]{2,1,0:T(8,128)S(1)}, f32[5,32,128]{2,1,0:T(8,128)S(1)}, u32[]{:S(2)}, u32[]{:S(2)}) collective-permute-start(f32[5,32,128]{2,1,0:T(8,128)S(1)} %get-tuple-element.53), channel_id=1, source_target_pairs={{0,120},{8,16},{16,8},{24,32},{32,24},{40,48},{48,40},{56,64},{64,... | collective-permute-start | bytes 245768 | tf_op jit(solution)/shard_map/ppermute | solution.py:460
  36.9 11.6 %collective-permute-start.9 = (f32[5,24,128]{2,1,0:T(8,128)S(1)}, f32[5,24,128]{2,1,0:T(8,128)S(1)}, u32[]{:S(2)}, u32[]{:S(2)}) collective-permute-start(f32[5,24,128]{2,1,0:T(8,128)S(1)} %shard_map.117), channel_id=1, source_target_pairs={{0,120},{8,112},{16,104},{24,96},{32,88},{40,80},{48,72},{56,64},{... | collective-permute-start | bytes 184328 | tf_op jit(solution)/shard_map/ppermute | solution.py:464
  37.0 7.5 %collective-permute-start.8 = (f32[5,8,128]{2,1,0:T(8,128)S(1)}, f32[5,8,128]{2,1,0:T(8,128)S(1)}, u32[]{:S(2)}, u32[]{:S(2)}) collective-permute-start(f32[5,8,128]{2,1,0:T(8,128)S(1)} %get-tuple-element.54), channel_id=1, source_target_pairs={{0,7},{1,2},{2,1},{3,4},{4,3},{5,6},{6,5},{7,0},{8,15},{9,10},{10,... | collective-permute-start | bytes 61448 | tf_op jit(solution)/shard_map/ppermute | solution.py:461
  39.2 5.5 %collective-permute-start.7 = (f32[5,8,128]{2,1,0:T(8,128)S(1)}, f32[5,8,128]{2,1,0:T(8,128)S(1)}, u32[]{:S(2)}, u32[]{:S(2)}) collective-permute-start(f32[5,8,128]{2,1,0:T(8,128)S(1)} %get-tuple-element.54), channel_id=1, source_target_pairs={{0,1},{1,0},{2,3},{3,2},{4,5},{5,4},{6,7},{7,6},{8,9},{9,8},{10,11... | collective-permute-start | bytes 61448 | tf_op jit(solution)/shard_map/ppermute | solution.py:462
  44.7 4.0 %copy-start.3 = (f32[3,5,16,128]{3,2,1,0:T(8,128)S(1)}, f32[3,5,16,128]{3,2,1,0:T(8,128)}, u32[]{:S(2)}) copy-start(f32[3,5,16,128]{3,2,1,0:T(8,128)} %refs_1_.1) | copy-start | bytes 368644
  44.7 4.0 %copy-start.5 = (s32[4,16,128]{2,1,0:T(8,128)S(1)}, s32[4,16,128]{2,1,0:T(8,128)}, u32[]{:S(2)}) copy-start(s32[4,16,128]{2,1,0:T(8,128)} %refs_3_.11) | copy-start | bytes 98308
  44.7 4.0 %copy-start.6 = (f32[4,16,128]{2,1,0:T(8,128)S(1)}, f32[4,16,128]{2,1,0:T(8,128)}, u32[]{:S(2)}) copy-start(f32[4,16,128]{2,1,0:T(8,128)} %refs_4_.11) | copy-start | bytes 98308
  49.8 6.2 %collective-permute-start.10 = (f32[7,32,128]{2,1,0:T(8,128)S(1)}, f32[7,32,128]{2,1,0:T(8,128)S(1)}, u32[]{:S(2)}, u32[]{:S(2)}) collective-permute-start(f32[7,32,128]{2,1,0:T(8,128)S(1)} %get-tuple-element.62), channel_id=1, source_target_pairs={{0,8},{8,0},{16,24},{24,16},{32,40},{40,32},{48,56},{56,48},{64,72... | collective-permute-start | bytes 344072 | tf_op jit(solution)/shard_map/ppermute | solution.py:459
  49.9 6.1 %collective-permute-start.11 = (f32[5,32,128]{2,1,0:T(8,128)S(1)}, f32[5,32,128]{2,1,0:T(8,128)S(1)}, u32[]{:S(2)}, u32[]{:S(2)}) collective-permute-start(f32[5,32,128]{2,1,0:T(8,128)S(1)} %get-tuple-element.63), channel_id=1, source_target_pairs={{0,120},{8,16},{16,8},{24,32},{32,24},{40,48},{48,40},{56,64},{64,... | collective-permute-start | bytes 245768 | tf_op jit(solution)/shard_map/ppermute | solution.py:460
  56.0 29.5 %collective-permute-start.14 = (f32[5,24,128]{2,1,0:T(8,128)S(1)}, f32[5,24,128]{2,1,0:T(8,128)S(1)}, u32[]{:S(2)}, u32[]{:S(2)}) collective-permute-start(f32[5,24,128]{2,1,0:T(8,128)S(1)} %shard_map.121), channel_id=1, source_target_pairs={{0,120},{8,112},{16,104},{24,96},{32,88},{40,80},{48,72},{56,64},{... | collective-permute-start | bytes 184328 | tf_op jit(solution)/shard_map/ppermute | solution.py:464
  58.5 3.8 %collective-permute-start.15 = (f32[4,8,128]{2,1,0:T(8,128)S(1)}, f32[4,8,128]{2,1,0:T(8,128)S(1)}, u32[]{:S(2)}, u32[]{:S(2)}) collective-permute-start(f32[4,8,128]{2,1,0:T(8,128)S(1)} %get-tuple-element.70), channel_id=1, source_target_pairs={{0,16},{1,17},{2,18},{3,19},{4,20},{5,21},{6,22},{7,23},{8,24},{9,... | collective-permute-start | bytes 49160 | tf_op jit(solution)/shard_map/ppermute | solution.py:422
  62.3 4.9 %collective-permute-start.16 = (f32[2,8,128]{2,1,0:T(8,128)S(1)}, f32[2,8,128]{2,1,0:T(8,128)S(1)}, u32[]{:S(2)}, u32[]{:S(2)}) collective-permute-start(f32[2,8,128]{2,1,0:T(8,128)S(1)} %get-tuple-element.72), channel_id=1, source_target_pairs={{0,48},{1,49},{2,50},{3,51},{4,52},{5,53},{6,54},{7,55},{8,56},{9,... | collective-permute-start | bytes 24584 | tf_op jit(solution)/shard_map/ppermute | solution.py:422
  62.3 18.4 %collective-permute-start.13 = (f32[5,8,128]{2,1,0:T(8,128)S(1)}, f32[5,8,128]{2,1,0:T(8,128)S(1)}, u32[]{:S(2)}, u32[]{:S(2)}) collective-permute-start(f32[5,8,128]{2,1,0:T(8,128)S(1)} %get-tuple-element.64), channel_id=1, source_target_pairs={{0,7},{1,2},{2,1},{3,4},{4,3},{5,6},{6,5},{7,0},{8,15},{9,10},{10,... | collective-permute-start | bytes 61448 | tf_op jit(solution)/shard_map/ppermute | solution.py:461
  66.2 14.5 %collective-permute-start.12 = (f32[5,8,128]{2,1,0:T(8,128)S(1)}, f32[5,8,128]{2,1,0:T(8,128)S(1)}, u32[]{:S(2)}, u32[]{:S(2)}) collective-permute-start(f32[5,8,128]{2,1,0:T(8,128)S(1)} %get-tuple-element.64), channel_id=1, source_target_pairs={{0,1},{1,0},{2,3},{3,2},{4,5},{5,4},{6,7},{7,6},{8,9},{9,8},{10,11... | collective-permute-start | bytes 61448 | tf_op jit(solution)/shard_map/ppermute | solution.py:462
  67.2 3.6 %collective-permute-start.17 = (f32[1,8,128]{2,1,0:T(8,128)S(1)}, f32[1,8,128]{2,1,0:T(8,128)S(1)}, u32[]{:S(2)}, u32[]{:S(2)}) collective-permute-start(f32[1,8,128]{2,1,0:T(8,128)S(1)} %get-tuple-element.74), channel_id=1, source_target_pairs={{0,64},{1,65},{2,66},{3,67},{4,68},{5,69},{6,70},{7,71},{8,72},{9,... | collective-permute-start | bytes 12296 | tf_op jit(solution)/shard_map/ppermute | solution.py:422
  70.8 4.8 %collective-permute-start.18 = (f32[1,8,128]{2,1,0:T(8,128)S(1)}, f32[1,8,128]{2,1,0:T(8,128)S(1)}, u32[]{:S(2)}, u32[]{:S(2)}) collective-permute-start(f32[1,8,128]{2,1,0:T(8,128)S(1)} %shard_map.126.a_ref), channel_id=1, source_target_pairs={{0,65},{1,64},{2,67},{3,66},{4,69},{5,68},{6,71},{7,70},{8,73},{9,... | collective-permute-start | bytes 12296 | tf_op jit(solution)/shard_map/ppermute | solution.py:422
  75.6 3.6 %collective-permute-start.19 = (f32[1,8,128]{2,1,0:T(8,128)S(1)}, f32[1,8,128]{2,1,0:T(8,128)S(1)}, u32[]{:S(2)}, u32[]{:S(2)}) collective-permute-start(f32[1,8,128]{2,1,0:T(8,128)S(1)} %shard_map.127.a_ref), channel_id=1, source_target_pairs={{0,2},{1,3},{2,0},{3,1},{4,6},{5,7},{6,4},{7,5},{8,10},{9,11},{10,... | collective-permute-start | bytes 12296 | tf_op jit(solution)/shard_map/ppermute | solution.py:422
  79.2 5.6 %collective-permute-start.20 = (f32[1,8,128]{2,1,0:T(8,128)S(1)}, f32[1,8,128]{2,1,0:T(8,128)S(1)}, u32[]{:S(2)}, u32[]{:S(2)}) collective-permute-start(f32[1,8,128]{2,1,0:T(8,128)S(1)} %shard_map.128.a_ref), channel_id=1, source_target_pairs={{0,6},{1,7},{2,4},{3,5},{4,2},{5,3},{6,0},{7,1},{8,14},{9,15},{10,... | collective-permute-start | bytes 12296 | tf_op jit(solution)/shard_map/ppermute | solution.py:422

commit v2 on v1

--- a/solution.py
+++ b/solution.py
@@ -72,11 +72,13 @@
 
 def first_faces(start_ref, v_ref, slab_ref, pair_ref, odd_ref, edge_ref, low_ref, high_ref, sem):
     lane = lane_index()
-    copy = pltpu.make_async_copy(start_ref, v_ref.at[:, :NJ], sem)
-    copy.start()
+    copies = []
+    for n in range(4):
+        at = pl.ds(n * 8, 8)
+        copies.append(pltpu.make_async_copy(start_ref.at[:, at], v_ref.at[:, at], sem.at[n]))
+        copies[-1].start()
     for c in range(COMPS):
         v_ref[c, NJ] = jnp.zeros((ROWS, LANES), F32)
-    copy.wait()
 
     def step(j, packed):
         halves = [(v_ref[c, j, :HALF], v_ref[c, j, HALF:]) for c in range(COMPS)]
@@ -85,9 +87,10 @@
             high_ref[c, pl.ds(j, 1)] = halves[c][1][HALF - 1 :]
         return tuple(pack_edges(list(packed), halves, j, lane))
 
-    packed = lax.fori_loop(
-        0, NJ, step, tuple(jnp.zeros((HALF, LANES), F32) for _ in range(COMPS)), unroll=4
-    )
+    packed = tuple(jnp.zeros((HALF, LANES), F32) for _ in range(COMPS))
+    for n in range(4):
+        copies[n].wait()
+        packed = lax.fori_loop(n * 8, n * 8 + 8, step, packed, unroll=8)
     for c in range(COMPS):
         edge_ref[c] = packed[c]
         slab_ref[c] = v_ref[c, 0]
@@ -402,8 +405,8 @@
     out_ref[...] = a_ref[...] + b_ref[...]
 
 
-def finish_points(a_ref, b_ref, out_ref):
-    total = a_ref[0] + b_ref[0]
+def finish_points(a_ref, b_ref, c_ref, d_ref, out_ref):
+    total = (a_ref[0] + b_ref[0]) + (c_ref[0] + d_ref[0])
     out_ref[...] = pltpu.roll(total, LANES - 8 * lax.axis_index("span"), 1)[:3, :8]
 
 
@@ -415,7 +418,7 @@
     ]
 
 
-FOLDS = (masked(2, 0), masked(6, 0), masked(8, 0), masked(8, 1), masked(0, 2), masked(0, 6))
+FOLDS = (masked(2, 0), masked(6, 0), masked(8, 0), masked(8, 1), masked(0, 2), masked(0, 6), masked(0, 4))
 
 
 def fold(x, n):
@@ -431,10 +434,11 @@
     args = (kept, fold(sent, 2))
     kept, sent = run_kernel(halve_lanes, tiles(1) * 2, args)
     got = fold(sent, 3)
-    for n in range(4, 7):
-        (kept,) = run_kernel(add_tiles, tiles(1), (kept, got))
-        got = fold(kept, n)
-    (out,) = run_kernel(finish_points, [shape_of(3, 8)], (kept, got))
+    (kept,) = run_kernel(add_tiles, tiles(1), (kept, got))
+    got = fold(kept, 4)
+    (kept,) = run_kernel(add_tiles, tiles(1), (kept, got))
+    others = [fold(kept, n) for n in (5, 6, 7)]
+    (out,) = run_kernel(finish_points, [shape_of(3, 8)], (kept, *others))
     return out
 
 
@@ -540,7 +544,7 @@
         first_faces,
         [shape_of(*d) for d in (TALL, SLAB, FACE, FACE, EDGE)],
         (pltpu.with_memory_space_constraint(adjoint_start, pltpu.HBM),),
-        scratch=(pltpu.VMEM(FACE, F32), pltpu.VMEM(FACE, F32), DMA),
+        scratch=(pltpu.VMEM(FACE, F32), pltpu.VMEM(FACE, F32), DMA((4,))),
         flops=1000000,
         far=(0,),
     )

time: 86.3 us -> 84.4 us (0.978)
  waiting for transfers between devices: 37.2 us -> 33.4 us
  starting transfers between devices: 29.3 us -> 31.8 us
    ppermute x6 -> x7, waiting for transfers between devices: 14.9 us -> 11 us  [fold(): return lax.ppermute(x, ('wrap', 'span'), FOLDS[n - 1])]
    ppermute x6 -> x7, starting transfers between devices: 3.41 us -> 5.89 us  [fold(): return lax.ppermute(x, ('wrap', 'span'), FOLDS[n - 1])]
    pallas_call x18 -> x17, Pallas kernels: 18.8 us -> 18.1 us  [run_kernel(): pl.pallas_call(kernel, out_shape=outs, in_specs=[FARSPEC if n in far else...]
  transfers between devices with their start and end apart: 21 -> 22, of which waited for: 13 -> 11; matrix products, arithmetic and copies ran while one was open for 0% -> 0% of each run, Pallas kernels for 17% -> 17%
where the time goes in v2:
time: 84.4 us; the launch traced here: 84.2 us
  waiting for transfers between devices  33.4 us (40%)
  starting transfers between devices  31.8 us (38%)
  Pallas kernels  18.1 us (21%)
  between operations  0.85 us (1%)
    pallas_call x17, Pallas kernels, run_kernel(): pl.pallas_call(kernel, out_shape=outs, in_specs=[FARSPEC if n in far else...  18.1 us
    ppermute x3, starting transfers between devices, exchange(): odd = lax.ppermute(edge, 'span', SPAN_ODD)  11.2 us
    ppermute x7, waiting for transfers between devices, fold(): return lax.ppermute(x, ('wrap', 'span'), FOLDS[n - 1])  11 us
    ppermute x3, waiting for transfers between devices, exchange(): far = lax.ppermute(odd_face, 'wrap', WRAP_ODD)  10.5 us
    ppermute x3, starting transfers between devices, exchange(): far = lax.ppermute(odd_face, 'wrap', WRAP_ODD)  7.83 us
    ppermute x3, waiting for transfers between devices, exchange(): odd = lax.ppermute(edge, 'span', SPAN_ODD)  7.48 us
    ppermute x3, starting transfers between devices, exchange(): window = lax.ppermute(rows, 'wrap', MIRROR)  6.5 us
    ppermute x7, starting transfers between devices, fold(): return lax.ppermute(x, ('wrap', 'span'), FOLDS[n - 1])  5.89 us
  transfers between devices with their start and end apart: 22, of which 11 were waited for; matrix products, arithmetic and copies ran while one was open for 0% of the time, Pallas kernels for 17%

profile of v2, /device:TPU:0, one launch (start us, length us, event | category | flops | bytes accessed | tf_op | source)
XLA Modules:
  0.0 84.2 jit_solution(3532125125466910775)
XLA Ops:
  0.7 1.8 %shard_map.112 = (f32[5,33,16,128]{3,2,1,0:T(8,128)S(1)}, f32[5,16,128]{2,1,0:T(8,128)S(1)}, f32[5,32,128]{2,1,0:T(8,128)S(1)}, f32[5,32,128]{2,1,0:T(8,128)S(1)}, f32[5,8,128]{2,1,0:T(8,128)S(1)}) custom-call(f32[5,32,16,128]{3,2,1,0:T(8,128)} %start_ref.1), custom_call_target="tpu_custom_call" | custom-call | flops 1000000 | bytes 1310720 | tf_op jit(solution)/shard_map/pallas_call | solution.py:33
  2.4 0.1 collective-permute-start
  2.5 5.3 %collective-permute-start.1 = (f32[5,32,128]{2,1,0:T(8,128)S(1)}, f32[5,32,128]{2,1,0:T(8,128)S(1)}, u32[]{:S(2)}, u32[]{:S(2)}) collective-permute-start(f32[5,32,128]{2,1,0:T(8,128)S(1)} %get-tuple-element.42), channel_id=1, source_target_pairs={{0,120},{8,16},{16,8},{24,32},{32,24},{40,48},{48,40},{56,64},{64,... | collective-permute-start | bytes 245768 | tf_op jit(solution)/shard_map/ppermute | solution.py:464
  7.8 2.1 %collective-permute-done.1.refs_6_.odd_ref = f32[5,32,128]{2,1,0:T(8,128)S(1)} collective-permute-done((f32[5,32,128]{2,1,0:T(8,128)S(1)}, f32[5,32,128]{2,1,0:T(8,128)S(1)}, u32[]{:S(2)}, u32[]{:S(2)}) %collective-permute-start.1) | collective-permute-done | bytes 81952 | tf_op jit(solution)/shard_map/ppermute | solution.py:464
  10.0 3.9 %collective-permute-start.4 = (f32[5,24,128]{2,1,0:T(8,128)S(1)}, f32[5,24,128]{2,1,0:T(8,128)S(1)}, u32[]{:S(2)}, u32[]{:S(2)}) collective-permute-start(f32[5,24,128]{2,1,0:T(8,128)S(1)} %shard_map.114), channel_id=1, source_target_pairs={{0,120},{8,112},{16,104},{24,96},{32,88},{40,80},{48,72},{56,64},{... | collective-permute-start | bytes 184328 | tf_op jit(solution)/shard_map/ppermute | solution.py:468
  13.9 5.1 %collective-permute-start.3 = (f32[5,8,128]{2,1,0:T(8,128)S(1)}, f32[5,8,128]{2,1,0:T(8,128)S(1)}, u32[]{:S(2)}, u32[]{:S(2)}) collective-permute-start(f32[5,8,128]{2,1,0:T(8,128)S(1)} %get-tuple-element.43), channel_id=1, source_target_pairs={{0,7},{1,2},{2,1},{3,4},{4,3},{5,6},{6,5},{7,0},{8,15},{9,10},{10,... | collective-permute-start | bytes 61448 | tf_op jit(solution)/shard_map/ppermute | solution.py:465
  19.0 0.0 collective-permute-start.2
  19.0 2.3 %collective-permute-done.3.refs_8_ = f32[5,8,128]{2,1,0:T(8,128)S(1)} collective-permute-done((f32[5,8,128]{2,1,0:T(8,128)S(1)}, f32[5,8,128]{2,1,0:T(8,128)S(1)}, u32[]{:S(2)}, u32[]{:S(2)}) %collective-permute-start.3) | collective-permute-done | bytes 20512 | tf_op jit(solution)/shard_map/ppermute | solution.py:465
  21.3 3.0 %collective-permute-done.2.refs_7_ = f32[5,8,128]{2,1,0:T(8,128)S(1)} collective-permute-done((f32[5,8,128]{2,1,0:T(8,128)S(1)}, f32[5,8,128]{2,1,0:T(8,128)S(1)}, u32[]{:S(2)}, u32[]{:S(2)}) %collective-permute-start.2) | collective-permute-done | bytes 20512 | tf_op jit(solution)/shard_map/ppermute | solution.py:466
  24.3 5.6 %shard_map.113 = (f32[5,33,16,128]{3,2,1,0:T(8,128)S(1)}, f32[5,16,128]{2,1,0:T(8,128)S(1)}, f32[5,32,128]{2,1,0:T(8,128)S(1)}, f32[5,32,128]{2,1,0:T(8,128)S(1)...) custom-call(f32[5,33,16,128]{3,2,1,0:T(8,128)S(1)} %get-tuple-element.39.refs_0_, ...), custom_call_target="tpu_custom_call" | custom-call | flops 52428800 | bytes 13000704 | tf_op jit(solution)/shard_map/pallas_call | solution.py:33
  29.9 0.0 collective-permute-done.4.refs_5_
  30.0 0.1 shard_map.115
  30.1 0.1 collective-permute-start.5
  30.2 0.1 collective-permute-start.6
  30.3 1.2 %collective-permute-done.5.refs_5_.pair_ref = f32[5,32,128]{2,1,0:T(8,128)S(1)} collective-permute-done((f32[5,32,128]{2,1,0:T(8,128)S(1)}, f32[5,32,128]{2,1,0:T(8,128)S(1)}, u32[]{:S(2)}, u32[]{:S(2)}) %collective-permute-start.5) | collective-permute-done | bytes 81952 | tf_op jit(solution)/shard_map/ppermute | solution.py:463
  31.4 4.8 %collective-permute-done.6.refs_6_.odd_ref = f32[5,32,128]{2,1,0:T(8,128)S(1)} collective-permute-done((f32[5,32,128]{2,1,0:T(8,128)S(1)}, f32[5,32,128]{2,1,0:T(8,128)S(1)}, u32[]{:S(2)}, u32[]{:S(2)}) %collective-permute-start.6) | collective-permute-done | bytes 81952 | tf_op jit(solution)/shard_map/ppermute | solution.py:464
  36.3 0.1 collective-permute-start.9
  36.4 2.2 %collective-permute-start.8 = (f32[5,8,128]{2,1,0:T(8,128)S(1)}, f32[5,8,128]{2,1,0:T(8,128)S(1)}, u32[]{:S(2)}, u32[]{:S(2)}) collective-permute-start(f32[5,8,128]{2,1,0:T(8,128)S(1)} %get-tuple-element.54), channel_id=1, source_target_pairs={{0,7},{1,2},{2,1},{3,4},{4,3},{5,6},{6,5},{7,0},{8,15},{9,10},{10,... | collective-permute-start | bytes 61448 | tf_op jit(solution)/shard_map/ppermute | solution.py:465
  38.6 0.1 collective-permute-start.7
  38.7 5.2 %collective-permute-done.8.refs_8_ = f32[5,8,128]{2,1,0:T(8,128)S(1)} collective-permute-done((f32[5,8,128]{2,1,0:T(8,128)S(1)}, f32[5,8,128]{2,1,0:T(8,128)S(1)}, u32[]{:S(2)}, u32[]{:S(2)}) %collective-permute-start.8) | collective-permute-done | bytes 20512 | tf_op jit(solution)/shard_map/ppermute | solution.py:465
  43.8 0.2 collective-permute-done.7.refs_7_
  44.1 3.8 %shard_map.116 = (f32[5,33,16,128]{3,2,1,0:T(8,128)S(1)}, f32[5,16,128]{2,1,0:T(8,128)S(1)}, f32[5,32,128]{2,1,0:T(8,128)S(1)}, f32[5,32,128]{2,1,0:T(8,128)S(1)}, f32[5,8,128]{2,1,0:T(8,128)S(1)}) custom-call(f32[5,33,16,128]{3,2,1,0:T(8,128)S(1)} %get-tuple-element.44.refs_0_, f32[5,16,128]{2,1,0:T(8,128)S(1)} %get-tuple-element.50.refs_1_.slab_ref.refs_0_, ...), custom_call_target="tpu_custom_call" | custom-call | flops 52428800 | bytes 22831104 | tf_op jit(solution)/shard_map/pallas_call | solution.py:33
  47.9 0.0 collective-permute-done.9.refs_5_
  47.9 0.1 shard_map.118
  48.1 1.1 %shard_map.119 = (f32[8,8,128]{2,1,0:T(8,128)S(1)}, f32[7,32,128]{2,1,0:T(8,128)S(1)}) custom-call(f32[5,16,128]{2,1,0:T(8,128)S(1)} %get-tuple-element.60.refs_0_.refs_1_.slab_ref, f32[3,5,16,128]{3,2,1,0:T(8,128)S(1)} %copy-done.3, s32[16,128]{1,0:T(8,128)S(1)} %copy-done.2, s32[4,16,128]{2,1,0:T(8,128)S(1)} %copy-done.5, f32[4,16,128]{2,1,0:T(8,128)S(1)} %copy-done.6, ...), custom_call_target="tpu_custom_call" | custom-call | flops 10000000 | bytes 319488 | tf_op jit(solution)/shard_map/pallas_call | solution.py:33
  49.2 0.1 collective-permute-start.10
  49.3 2.5 %collective-permute-start.11 = (f32[5,32,128]{2,1,0:T(8,128)S(1)}, f32[5,32,128]{2,1,0:T(8,128)S(1)}, u32[]{:S(2)}, u32[]{:S(2)}) collective-permute-start(f32[5,32,128]{2,1,0:T(8,128)S(1)} %get-tuple-element.63), channel_id=1, source_target_pairs={{0,120},{8,16},{16,8},{24,32},{32,24},{40,48},{48,40},{56,64},{64,... | collective-permute-start | bytes 245768 | tf_op jit(solution)/shard_map/ppermute | solution.py:464
  51.8 3.6 %collective-permute-done.11.refs_6_.odd_ref = f32[5,32,128]{2,1,0:T(8,128)S(1)} collective-permute-done((f32[5,32,128]{2,1,0:T(8,128)S(1)}, f32[5,32,128]{2,1,0:T(8,128)S(1)}, u32[]{:S(2)}, u32[]{:S(2)}) %collective-permute-start.11) | collective-permute-done | bytes 81952 | tf_op jit(solution)/shard_map/ppermute | solution.py:464
  55.3 0.0 collective-permute-done.10.refs_5_.pair_ref.bundle_ref
  55.4 2.5 %collective-permute-start.14 = (f32[5,24,128]{2,1,0:T(8,128)S(1)}, f32[5,24,128]{2,1,0:T(8,128)S(1)}, u32[]{:S(2)}, u32[]{:S(2)}) collective-permute-start(f32[5,24,128]{2,1,0:T(8,128)S(1)} %shard_map.121), channel_id=1, source_target_pairs={{0,120},{8,112},{16,104},{24,96},{32,88},{40,80},{48,72},{56,64},{... | collective-permute-start | bytes 184328 | tf_op jit(solution)/shard_map/ppermute | solution.py:468
  57.9 0.1 collective-permute-start.15
  58.0 3.9 %collective-permute-start.13 = (f32[5,8,128]{2,1,0:T(8,128)S(1)}, f32[5,8,128]{2,1,0:T(8,128)S(1)}, u32[]{:S(2)}, u32[]{:S(2)}) collective-permute-start(f32[5,8,128]{2,1,0:T(8,128)S(1)} %get-tuple-element.64), channel_id=1, source_target_pairs={{0,7},{1,2},{2,1},{3,4},{4,3},{5,6},{6,5},{7,0},{8,15},{9,10},{10,... | collective-permute-start | bytes 61448 | tf_op jit(solution)/shard_map/ppermute | solution.py:465
  61.9 0.0 collective-permute-start.12
  61.9 0.0 collective-permute-done.15.got_ref
  61.9 0.1 collective-permute-start.16
  62.0 4.8 %collective-permute-done.16.got_ref = f32[2,8,128]{2,1,0:T(8,128)S(1)} collective-permute-done((f32[2,8,128]{2,1,0:T(8,128)S(1)}, f32[2,8,128]{2,1,0:T(8,128)S(1)}, u32[]{:S(2)}, u32[]{:S(2)}) %collective-permute-start.16) | collective-permute-done | bytes 8224 | tf_op jit(solution)/shard_map/ppermute | solution.py:425
  66.9 0.2 collective-permute-start.17
  67.0 3.4 %collective-permute-done.17.b_ref = f32[1,8,128]{2,1,0:T(8,128)S(1)} collective-permute-done((f32[1,8,128]{2,1,0:T(8,128)S(1)}, f32[1,8,128]{2,1,0:T(8,128)S(1)}, u32[]{:S(2)}, u32[]{:S(2)}) %collective-permute-start.17) | collective-permute-done | bytes 4128 | tf_op jit(solution)/shard_map/ppermute | solution.py:425
  70.5 2.1 %collective-permute-start.18 = (f32[1,8,128]{2,1,0:T(8,128)S(1)}, f32[1,8,128]{2,1,0:T(8,128)S(1)}, u32[]{:S(2)}, u32[]{:S(2)}) collective-permute-start(f32[1,8,128]{2,1,0:T(8,128)S(1)} %shard_map.126.a_ref), channel_id=1, source_target_pairs={{0,65},{1,64},{2,67},{3,66},{4,69},{5,68},{6,71},{7,70},{8,73},{9,... | collective-permute-start | bytes 12296 | tf_op jit(solution)/shard_map/ppermute | solution.py:425
  72.5 2.8 %collective-permute-done.18.b_ref = f32[1,8,128]{2,1,0:T(8,128)S(1)} collective-permute-done((f32[1,8,128]{2,1,0:T(8,128)S(1)}, f32[1,8,128]{2,1,0:T(8,128)S(1)}, u32[]{:S(2)}, u32[]{:S(2)}) %collective-permute-start.18) | collective-permute-done | bytes 4128 | tf_op jit(solution)/shard_map/ppermute | solution.py:425
  75.3 1.1 %collective-permute-start.21 = (f32[1,8,128]{2,1,0:T(8,128)S(1)}, f32[1,8,128]{2,1,0:T(8,128)S(1)}, u32[]{:S(2)}, u32[]{:S(2)}) collective-permute-start(f32[1,8,128]{2,1,0:T(8,128)S(1)} %shard_map.127.a_ref), channel_id=1, source_target_pairs={{0,4},{1,5},{2,6},{3,7},{4,0},{5,1},{6,2},{7,3},{8,12},{9,13},{10,... | collective-permute-start | bytes 12296 | tf_op jit(solution)/shard_map/ppermute | solution.py:425
  76.4 1.2 %collective-permute-start.20 = (f32[1,8,128]{2,1,0:T(8,128)S(1)}, f32[1,8,128]{2,1,0:T(8,128)S(1)}, u32[]{:S(2)}, u32[]{:S(2)}) collective-permute-start(f32[1,8,128]{2,1,0:T(8,128)S(1)} %shard_map.127.a_ref), channel_id=1, source_target_pairs={{0,6},{1,7},{2,4},{3,5},{4,2},{5,3},{6,0},{7,1},{8,14},{9,15},{10,... | collective-permute-start | bytes 12296 | tf_op jit(solution)/shard_map/ppermute | solution.py:425
  77.7 1.1 %collective-permute-start.19 = (f32[1,8,128]{2,1,0:T(8,128)S(1)}, f32[1,8,128]{2,1,0:T(8,128)S(1)}, u32[]{:S(2)}, u32[]{:S(2)}) collective-permute-start(f32[1,8,128]{2,1,0:T(8,128)S(1)} %shard_map.127.a_ref), channel_id=1, source_target_pairs={{0,2},{1,3},{2,0},{3,1},{4,6},{5,7},{6,4},{7,5},{8,10},{9,11},{10,... | collective-permute-start | bytes 12296 | tf_op jit(solution)/shard_map/ppermute | solution.py:425
  78.8 4.1 %shard_map.120 = (f32[5,32,16,128]{3,2,1,0:T(8,128)}, f32[5,16,128]{2,1,0:T(8,128)S(1)}, f32[5,32,16,128]{3,2,1,0:T(8,128)}) custom-call(f32[5,33,16,128]{3,2,1,0:T(8,128)S(1)} %get-tuple-element.55.refs_0_, f32[5,16,128]{2,1,0:T(8,128)S(1)} %get-tuple-element.60.refs_0_.refs_1_.slab_ref, f32[3,5,5,32,16,128]{5,4,3,2,1,0:T(8,128)S(1)} %get-tuple-element.51.refs_2_, ...), custom_call_target="tpu_custom_call" | custom-call | flops 52428800 | bytes 22863872 | tf_op jit(solution)/shard_map/pallas_call | solution.py:33
  82.9 0.0 collective-permute-done.21.d_ref
  82.9 0.0 collective-permute-done.19.b_ref
  82.9 0.7 shard_map.128
  83.6 0.7 shard_map.122
  (27 shorter events, 0.2 us)
Async XLA Ops:
  0.6 23.6 %copy-start.1 = (f32[32,16,128]{2,1,0:T(8,128)S(1)}, f32[32,16,128]{2,1,0:T(8,128)}, u32[]{:S(2)}) copy-start(f32[32,16,128]{2,1,0:T(8,128)} %refs_2_.9) | copy-start | bytes 786436
  0.6 23.6 %copy-start = (f32[5,32,16,128]{3,2,1,0:T(8,128)S(1)}, f32[5,32,16,128]{3,2,1,0:T(8,128)}, u32[]{:S(2)}) copy-start(f32[5,32,16,128]{3,2,1,0:T(8,128)} %refs_3_.12) | copy-start | bytes 3932164
  2.4 5.4 %collective-permute-start = (f32[5,32,128]{2,1,0:T(8,128)S(1)}, f32[5,32,128]{2,1,0:T(8,128)S(1)}, u32[]{:S(2)}, u32[]{:S(2)}) collective-permute-start(f32[5,32,128]{2,1,0:T(8,128)S(1)} %get-tuple-element.41), channel_id=1, source_target_pairs={{0,8},{8,0},{16,24},{24,16},{32,40},{40,32},{48,56},{56,48},{64,72... | collective-permute-start | bytes 245768 | tf_op jit(solution)/shard_map/ppermute | solution.py:463
  2.5 7.4 %collective-permute-start.1 = (f32[5,32,128]{2,1,0:T(8,128)S(1)}, f32[5,32,128]{2,1,0:T(8,128)S(1)}, u32[]{:S(2)}, u32[]{:S(2)}) collective-permute-start(f32[5,32,128]{2,1,0:T(8,128)S(1)} %get-tuple-element.42), channel_id=1, source_target_pairs={{0,120},{8,16},{16,8},{24,32},{32,24},{40,48},{48,40},{56,64},{64,... | collective-permute-start | bytes 245768 | tf_op jit(solution)/shard_map/ppermute | solution.py:464
  10.0 20.0 %collective-permute-start.4 = (f32[5,24,128]{2,1,0:T(8,128)S(1)}, f32[5,24,128]{2,1,0:T(8,128)S(1)}, u32[]{:S(2)}, u32[]{:S(2)}) collective-permute-start(f32[5,24,128]{2,1,0:T(8,128)S(1)} %shard_map.114), channel_id=1, source_target_pairs={{0,120},{8,112},{16,104},{24,96},{32,88},{40,80},{48,72},{56,64},{... | collective-permute-start | bytes 184328 | tf_op jit(solution)/shard_map/ppermute | solution.py:468
  13.9 7.4 %collective-permute-start.3 = (f32[5,8,128]{2,1,0:T(8,128)S(1)}, f32[5,8,128]{2,1,0:T(8,128)S(1)}, u32[]{:S(2)}, u32[]{:S(2)}) collective-permute-start(f32[5,8,128]{2,1,0:T(8,128)S(1)} %get-tuple-element.43), channel_id=1, source_target_pairs={{0,7},{1,2},{2,1},{3,4},{4,3},{5,6},{6,5},{7,0},{8,15},{9,10},{10,... | collective-permute-start | bytes 61448 | tf_op jit(solution)/shard_map/ppermute | solution.py:465
  19.0 5.3 %collective-permute-start.2 = (f32[5,8,128]{2,1,0:T(8,128)S(1)}, f32[5,8,128]{2,1,0:T(8,128)S(1)}, u32[]{:S(2)}, u32[]{:S(2)}) collective-permute-start(f32[5,8,128]{2,1,0:T(8,128)S(1)} %get-tuple-element.43), channel_id=1, source_target_pairs={{0,1},{1,0},{2,3},{3,2},{4,5},{5,4},{6,7},{7,6},{8,9},{9,8},{10,11... | collective-permute-start | bytes 61448 | tf_op jit(solution)/shard_map/ppermute | solution.py:466
  24.3 5.7 %copy-start.2 = (s32[16,128]{1,0:T(8,128)S(1)}, s32[16,128]{1,0:T(8,128)}, u32[]{:S(2)}) copy-start(s32[16,128]{1,0:T(8,128)} %refs_3_.13) | copy-start | bytes 24580
  24.3 5.7 %copy-start.4 = (s32[16,128]{1,0:T(8,128)S(1)}, s32[16,128]{1,0:T(8,128)}, u32[]{:S(2)}) copy-start(s32[16,128]{1,0:T(8,128)} %refs_4_.13) | copy-start | bytes 24580
  30.1 1.3 %collective-permute-start.5 = (f32[5,32,128]{2,1,0:T(8,128)S(1)}, f32[5,32,128]{2,1,0:T(8,128)S(1)}, u32[]{:S(2)}, u32[]{:S(2)}) collective-permute-start(f32[5,32,128]{2,1,0:T(8,128)S(1)} %get-tuple-element.52), channel_id=1, source_target_pairs={{0,8},{8,0},{16,24},{24,16},{32,40},{40,32},{48,56},{56,48},{64,72... | collective-permute-start | bytes 245768 | tf_op jit(solution)/shard_map/ppermute | solution.py:463
  30.2 6.1 %collective-permute-start.6 = (f32[5,32,128]{2,1,0:T(8,128)S(1)}, f32[5,32,128]{2,1,0:T(8,128)S(1)}, u32[]{:S(2)}, u32[]{:S(2)}) collective-permute-start(f32[5,32,128]{2,1,0:T(8,128)S(1)} %get-tuple-element.53), channel_id=1, source_target_pairs={{0,120},{8,16},{16,8},{24,32},{32,24},{40,48},{48,40},{56,64},{64,... | collective-permute-start | bytes 245768 | tf_op jit(solution)/shard_map/ppermute | solution.py:464
  36.3 11.6 %collective-permute-start.9 = (f32[5,24,128]{2,1,0:T(8,128)S(1)}, f32[5,24,128]{2,1,0:T(8,128)S(1)}, u32[]{:S(2)}, u32[]{:S(2)}) collective-permute-start(f32[5,24,128]{2,1,0:T(8,128)S(1)} %shard_map.117), channel_id=1, source_target_pairs={{0,120},{8,112},{16,104},{24,96},{32,88},{40,80},{48,72},{56,64},{... | collective-permute-start | bytes 184328 | tf_op jit(solution)/shard_map/ppermute | solution.py:468
  36.4 7.5 %collective-permute-start.8 = (f32[5,8,128]{2,1,0:T(8,128)S(1)}, f32[5,8,128]{2,1,0:T(8,128)S(1)}, u32[]{:S(2)}, u32[]{:S(2)}) collective-permute-start(f32[5,8,128]{2,1,0:T(8,128)S(1)} %get-tuple-element.54), channel_id=1, source_target_pairs={{0,7},{1,2},{2,1},{3,4},{4,3},{5,6},{6,5},{7,0},{8,15},{9,10},{10,... | collective-permute-start | bytes 61448 | tf_op jit(solution)/shard_map/ppermute | solution.py:465
  38.6 5.5 %collective-permute-start.7 = (f32[5,8,128]{2,1,0:T(8,128)S(1)}, f32[5,8,128]{2,1,0:T(8,128)S(1)}, u32[]{:S(2)}, u32[]{:S(2)}) collective-permute-start(f32[5,8,128]{2,1,0:T(8,128)S(1)} %get-tuple-element.54), channel_id=1, source_target_pairs={{0,1},{1,0},{2,3},{3,2},{4,5},{5,4},{6,7},{7,6},{8,9},{9,8},{10,11... | collective-permute-start | bytes 61448 | tf_op jit(solution)/shard_map/ppermute | solution.py:466
  44.0 4.0 %copy-start.3 = (f32[3,5,16,128]{3,2,1,0:T(8,128)S(1)}, f32[3,5,16,128]{3,2,1,0:T(8,128)}, u32[]{:S(2)}) copy-start(f32[3,5,16,128]{3,2,1,0:T(8,128)} %refs_1_.1) | copy-start | bytes 368644
  44.1 4.0 %copy-start.5 = (s32[4,16,128]{2,1,0:T(8,128)S(1)}, s32[4,16,128]{2,1,0:T(8,128)}, u32[]{:S(2)}) copy-start(s32[4,16,128]{2,1,0:T(8,128)} %refs_3_.11) | copy-start | bytes 98308
  44.1 4.0 %copy-start.6 = (f32[4,16,128]{2,1,0:T(8,128)S(1)}, f32[4,16,128]{2,1,0:T(8,128)}, u32[]{:S(2)}) copy-start(f32[4,16,128]{2,1,0:T(8,128)} %refs_4_.11) | copy-start | bytes 98308
  49.2 6.2 %collective-permute-start.10 = (f32[7,32,128]{2,1,0:T(8,128)S(1)}, f32[7,32,128]{2,1,0:T(8,128)S(1)}, u32[]{:S(2)}, u32[]{:S(2)}) collective-permute-start(f32[7,32,128]{2,1,0:T(8,128)S(1)} %get-tuple-element.62), channel_id=1, source_target_pairs={{0,8},{8,0},{16,24},{24,16},{32,40},{40,32},{48,56},{56,48},{64,72... | collective-permute-start | bytes 344072 | tf_op jit(solution)/shard_map/ppermute | solution.py:463
  49.3 6.1 %collective-permute-start.11 = (f32[5,32,128]{2,1,0:T(8,128)S(1)}, f32[5,32,128]{2,1,0:T(8,128)S(1)}, u32[]{:S(2)}, u32[]{:S(2)}) collective-permute-start(f32[5,32,128]{2,1,0:T(8,128)S(1)} %get-tuple-element.63), channel_id=1, source_target_pairs={{0,120},{8,16},{16,8},{24,32},{32,24},{40,48},{48,40},{56,64},{64,... | collective-permute-start | bytes 245768 | tf_op jit(solution)/shard_map/ppermute | solution.py:464
  55.4 28.2 %collective-permute-start.14 = (f32[5,24,128]{2,1,0:T(8,128)S(1)}, f32[5,24,128]{2,1,0:T(8,128)S(1)}, u32[]{:S(2)}, u32[]{:S(2)}) collective-permute-start(f32[5,24,128]{2,1,0:T(8,128)S(1)} %shard_map.121), channel_id=1, source_target_pairs={{0,120},{8,112},{16,104},{24,96},{32,88},{40,80},{48,72},{56,64},{... | collective-permute-start | bytes 184328 | tf_op jit(solution)/shard_map/ppermute | solution.py:468
  57.9 4.0 %collective-permute-start.15 = (f32[4,8,128]{2,1,0:T(8,128)S(1)}, f32[4,8,128]{2,1,0:T(8,128)S(1)}, u32[]{:S(2)}, u32[]{:S(2)}) collective-permute-start(f32[4,8,128]{2,1,0:T(8,128)S(1)} %get-tuple-element.70), channel_id=1, source_target_pairs={{0,16},{1,17},{2,18},{3,19},{4,20},{5,21},{6,22},{7,23},{8,24},{9,... | collective-permute-start | bytes 49160 | tf_op jit(solution)/shard_map/ppermute | solution.py:425
  58.0 19.7 %collective-permute-start.13 = (f32[5,8,128]{2,1,0:T(8,128)S(1)}, f32[5,8,128]{2,1,0:T(8,128)S(1)}, u32[]{:S(2)}, u32[]{:S(2)}) collective-permute-start(f32[5,8,128]{2,1,0:T(8,128)S(1)} %get-tuple-element.64), channel_id=1, source_target_pairs={{0,7},{1,2},{2,1},{3,4},{4,3},{5,6},{6,5},{7,0},{8,15},{9,10},{10,... | collective-permute-start | bytes 61448 | tf_op jit(solution)/shard_map/ppermute | solution.py:465
  61.9 16.9 %collective-permute-start.12 = (f32[5,8,128]{2,1,0:T(8,128)S(1)}, f32[5,8,128]{2,1,0:T(8,128)S(1)}, u32[]{:S(2)}, u32[]{:S(2)}) collective-permute-start(f32[5,8,128]{2,1,0:T(8,128)S(1)} %get-tuple-element.64), channel_id=1, source_target_pairs={{0,1},{1,0},{2,3},{3,2},{4,5},{5,4},{6,7},{7,6},{8,9},{9,8},{10,11... | collective-permute-start | bytes 61448 | tf_op jit(solution)/shard_map/ppermute | solution.py:466
  61.9 4.9 %collective-permute-start.16 = (f32[2,8,128]{2,1,0:T(8,128)S(1)}, f32[2,8,128]{2,1,0:T(8,128)S(1)}, u32[]{:S(2)}, u32[]{:S(2)}) collective-permute-start(f32[2,8,128]{2,1,0:T(8,128)S(1)} %get-tuple-element.72), channel_id=1, source_target_pairs={{0,48},{1,49},{2,50},{3,51},{4,52},{5,53},{6,54},{7,55},{8,56},{9,... | collective-permute-start | bytes 24584 | tf_op jit(solution)/shard_map/ppermute | solution.py:425
  66.9 3.6 %collective-permute-start.17 = (f32[1,8,128]{2,1,0:T(8,128)S(1)}, f32[1,8,128]{2,1,0:T(8,128)S(1)}, u32[]{:S(2)}, u32[]{:S(2)}) collective-permute-start(f32[1,8,128]{2,1,0:T(8,128)S(1)} %get-tuple-element.74), channel_id=1, source_target_pairs={{0,64},{1,65},{2,66},{3,67},{4,68},{5,69},{6,70},{7,71},{8,72},{9,... | collective-permute-start | bytes 12296 | tf_op jit(solution)/shard_map/ppermute | solution.py:425
  70.5 4.8 %collective-permute-start.18 = (f32[1,8,128]{2,1,0:T(8,128)S(1)}, f32[1,8,128]{2,1,0:T(8,128)S(1)}, u32[]{:S(2)}, u32[]{:S(2)}) collective-permute-start(f32[1,8,128]{2,1,0:T(8,128)S(1)} %shard_map.126.a_ref), channel_id=1, source_target_pairs={{0,65},{1,64},{2,67},{3,66},{4,69},{5,68},{6,71},{7,70},{8,73},{9,... | collective-permute-start | bytes 12296 | tf_op jit(solution)/shard_map/ppermute | solution.py:425
  75.3 7.6 %collective-permute-start.21 = (f32[1,8,128]{2,1,0:T(8,128)S(1)}, f32[1,8,128]{2,1,0:T(8,128)S(1)}, u32[]{:S(2)}, u32[]{:S(2)}) collective-permute-start(f32[1,8,128]{2,1,0:T(8,128)S(1)} %shard_map.127.a_ref), channel_id=1, source_target_pairs={{0,4},{1,5},{2,6},{3,7},{4,0},{5,1},{6,2},{7,3},{8,12},{9,13},{10,... | collective-permute-start | bytes 12296 | tf_op jit(solution)/shard_map/ppermute | solution.py:425
  76.4 6.4 %collective-permute-start.20 = (f32[1,8,128]{2,1,0:T(8,128)S(1)}, f32[1,8,128]{2,1,0:T(8,128)S(1)}, u32[]{:S(2)}, u32[]{:S(2)}) collective-permute-start(f32[1,8,128]{2,1,0:T(8,128)S(1)} %shard_map.127.a_ref), channel_id=1, source_target_pairs={{0,6},{1,7},{2,4},{3,5},{4,2},{5,3},{6,0},{7,1},{8,14},{9,15},{10,... | collective-permute-start | bytes 12296 | tf_op jit(solution)/shard_map/ppermute | solution.py:425
  77.7 5.2 %collective-permute-start.19 = (f32[1,8,128]{2,1,0:T(8,128)S(1)}, f32[1,8,128]{2,1,0:T(8,128)S(1)}, u32[]{:S(2)}, u32[]{:S(2)}) collective-permute-start(f32[1,8,128]{2,1,0:T(8,128)S(1)} %shard_map.127.a_ref), channel_id=1, source_target_pairs={{0,2},{1,3},{2,0},{3,1},{4,6},{5,7},{6,4},{7,5},{8,10},{9,11},{10,... | collective-permute-start | bytes 12296 | tf_op jit(solution)/shard_map/ppermute | solution.py:425

commit v3 on v2

--- a/solution.py
+++ b/solution.py
@@ -110,7 +110,9 @@
 
 CHUNK = 4
 CHUNKS = NJ // CHUNK
-AHEAD = 3
+PIECE = 2
+PIECES = NJ // PIECE
+AHEAD = 5
 
 
 def apply_blocks(stage, *refs):
@@ -126,7 +128,7 @@
         far_ref, part_ref, final_ref, q_ref, before_ref, after_ref, out_ref, sems = refs[9:]
 
     def block_copy(n):
-        at = pl.ds(n * CHUNK, CHUNK)
+        at = pl.ds(n * PIECE, PIECE)
         return pltpu.make_async_copy(
             jac_ref.at[:, :, :, at], narrow_ref.at[:, :, :, at], sems.at[n]
         )
@@ -233,14 +235,12 @@
         j = 2 * t + 2
         if stage == 0:
 
-            @pl.when(j % CHUNK == 0)
+            n = t + 1
+            block_copy(n).wait()
+
+            @pl.when(n + AHEAD < PIECES)
             def _():
-                n = j // CHUNK
-                block_copy(n).wait()
-
-                @pl.when(n + AHEAD < CHUNKS)
-                def _():
-                    block_copy(n + AHEAD).start()
+                block_copy(n + AHEAD).start()
 
         packed = pack(j - 1, packed)
         prepare(j + 1, odd_stage_ref)
@@ -445,7 +445,15 @@
 WRAP_PAIR = [(i, i ^ 1) for i in range(WRAP)]
 WRAP_ODD = [(i, (i + 1) % WRAP if i % 2 else (i - 1) % WRAP) for i in range(WRAP)]
 SPAN_PAIR = [(i, i ^ 1) for i in range(SPAN)]
-SPAN_ODD = [(i, (i + 1) % SPAN if i % 2 else (i - 1) % SPAN) for i in range(SPAN)]
+
+
+def odd_partner(w, s):
+    if s in (0, SPAN - 1):
+        return (w ^ 1) * SPAN + s
+    return w * SPAN + (s + 1 if s % 2 else s - 1)
+
+
+SPAN_ODD = [(w * SPAN + s, odd_partner(w, s)) for w in range(WRAP) for s in range(SPAN)]
 MIRROR = [(i, WRAP - 1 - i) for i in range(WRAP)]
 
 FIELD = (COMPS, NJ, ROWS, LANES)
@@ -462,7 +470,7 @@
 def exchange(slab, pair_face, odd_face, edge):
     near = lax.ppermute(pair_face, "wrap", WRAP_PAIR)
     far = lax.ppermute(odd_face, "wrap", WRAP_ODD)
-    odd = lax.ppermute(edge, "span", SPAN_ODD)
+    odd = lax.ppermute(edge, ("wrap", "span"), SPAN_ODD)
     pair = lax.ppermute(edge, "span", SPAN_PAIR)
     (rows,) = run_kernel(mirror_rows, [shape_of(COMPS, 24, LANES)], (slab, near, far))
     window = lax.ppermute(rows, "wrap", MIRROR)
@@ -479,7 +487,7 @@
         scratch = [pltpu.VMEM(EDGE, F32), pltpu.VMEM(FACE, F32), pltpu.VMEM(FACE, F32)]
         if stage == 0:
             outs += [shape_of(*BLOCKS), shape_of(*BLOCKS[1:3], ROWS, LANES)]
-            scratch += [pltpu.VMEM(BLOCKS, BF16), DMA((CHUNKS,))]
+            scratch += [pltpu.VMEM(BLOCKS, BF16), DMA((PIECES,))]
         scratch += [pltpu.VMEM(STAGE, F32)] * 2
         v, part, *rest = run_kernel(
             kernel,

time: 84.4 us -> 82.7 us (0.980)
  waiting for transfers between devices: 33.4 us -> 25.7 us
  starting transfers between devices: 31.8 us -> 37.5 us
    ppermute x3, starting transfers between devices: 0.12 us -> 15.5 us  [exchange(): pair = lax.ppermute(edge, 'span', SPAN_PAIR)]
    ppermute x3, starting transfers between devices: 11.2 us -> 0.17 us  [exchange(): odd = lax.ppermute(edge, ('wrap', 'span'), SPAN_ODD)]
    ppermute x3, waiting for transfers between devices: 7.48 us -> 0.01 us  [exchange(): odd = lax.ppermute(edge, ('wrap', 'span'), SPAN_ODD)]
    ppermute x7, starting transfers between devices: 5.89 us -> 6.86 us  [fold(): return lax.ppermute(x, ('wrap', 'span'), FOLDS[n - 1])]
  transfers between devices with their start and end apart: 22 -> 22, of which waited for: 11 -> 9; matrix products, arithmetic and copies ran while one was open for 0% -> 0% of each run, Pallas kernels for 17% -> 17%
where the time goes in v3:
time: 82.7 us; the launch traced here: 82.1 us
  starting transfers between devices  37.5 us (45%)
  waiting for transfers between devices  25.7 us (31%)
  Pallas kernels  18 us (22%)
  between operations  0.87 us (1%)
    pallas_call x17, Pallas kernels, run_kernel(): pl.pallas_call(kernel, out_shape=outs, in_specs=[FARSPEC if n in far else...  18 us
    ppermute x3, starting transfers between devices, exchange(): pair = lax.ppermute(edge, 'span', SPAN_PAIR)  15.5 us
    ppermute x7, waiting for transfers between devices, fold(): return lax.ppermute(x, ('wrap', 'span'), FOLDS[n - 1])  10.8 us
    ppermute x3, waiting for transfers between devices, exchange(): far = lax.ppermute(odd_face, 'wrap', WRAP_ODD)  10.3 us
    ppermute x3, starting transfers between devices, exchange(): far = lax.ppermute(odd_face, 'wrap', WRAP_ODD)  8.04 us
    ppermute x7, starting transfers between devices, fold(): return lax.ppermute(x, ('wrap', 'span'), FOLDS[n - 1])  6.86 us
    ppermute x3, starting transfers between devices, exchange(): window = lax.ppermute(rows, 'wrap', MIRROR)  6.71 us
    ppermute x3, waiting for transfers between devices, exchange(): pair = lax.ppermute(edge, 'span', SPAN_PAIR)  3.51 us
  transfers between devices with their start and end apart: 22, of which 9 were waited for; matrix products, arithmetic and copies ran while one was open for 0% of the time, Pallas kernels for 17%

profile of v3, /device:TPU:0, one launch (start us, length us, event | category | flops | bytes accessed | tf_op | source)
XLA Modules:
  0.0 82.1 jit_solution(2205998240185534569)
XLA Ops:
  0.7 1.8 %shard_map.112 = (f32[5,33,16,128]{3,2,1,0:T(8,128)S(1)}, f32[5,16,128]{2,1,0:T(8,128)S(1)}, f32[5,32,128]{2,1,0:T(8,128)S(1)}, f32[5,32,128]{2,1,0:T(8,128)S(1)}, f32[5,8,128]{2,1,0:T(8,128)S(1)}) custom-call(f32[5,32,16,128]{3,2,1,0:T(8,128)} %start_ref.1), custom_call_target="tpu_custom_call" | custom-call | flops 1000000 | bytes 1310720 | tf_op jit(solution)/shard_map/pallas_call | solution.py:33
  2.4 0.1 collective-permute-start
  2.5 5.3 %collective-permute-start.1 = (f32[5,32,128]{2,1,0:T(8,128)S(1)}, f32[5,32,128]{2,1,0:T(8,128)S(1)}, u32[]{:S(2)}, u32[]{:S(2)}) collective-permute-start(f32[5,32,128]{2,1,0:T(8,128)S(1)} %get-tuple-element.42), channel_id=1, source_target_pairs={{0,120},{8,16},{16,8},{24,32},{32,24},{40,48},{48,40},{56,64},{64,... | collective-permute-start | bytes 245768 | tf_op jit(solution)/shard_map/ppermute | solution.py:472
  7.8 0.0 collective-permute-done.refs_5_.pair_ref
  7.8 2.1 %collective-permute-done.1.refs_6_.odd_ref = f32[5,32,128]{2,1,0:T(8,128)S(1)} collective-permute-done((f32[5,32,128]{2,1,0:T(8,128)S(1)}, f32[5,32,128]{2,1,0:T(8,128)S(1)}, u32[]{:S(2)}, u32[]{:S(2)}) %collective-permute-start.1) | collective-permute-done | bytes 81952 | tf_op jit(solution)/shard_map/ppermute | solution.py:472
  10.0 3.9 %collective-permute-start.4 = (f32[5,24,128]{2,1,0:T(8,128)S(1)}, f32[5,24,128]{2,1,0:T(8,128)S(1)}, u32[]{:S(2)}, u32[]{:S(2)}) collective-permute-start(f32[5,24,128]{2,1,0:T(8,128)S(1)} %shard_map.114), channel_id=1, source_target_pairs={{0,120},{8,112},{16,104},{24,96},{32,88},{40,80},{48,72},{56,64},{... | collective-permute-start | bytes 184328 | tf_op jit(solution)/shard_map/ppermute | solution.py:476
  13.9 0.0 collective-permute-start.3
  13.9 4.5 %collective-permute-start.2 = (f32[5,8,128]{2,1,0:T(8,128)S(1)}, f32[5,8,128]{2,1,0:T(8,128)S(1)}, u32[]{:S(2)}, u32[]{:S(2)}) collective-permute-start(f32[5,8,128]{2,1,0:T(8,128)S(1)} %get-tuple-element.43), channel_id=1, source_target_pairs={{0,1},{1,0},{2,3},{3,2},{4,5},{5,4},{6,7},{7,6},{8,9},{9,8},{10,11... | collective-permute-start | bytes 61448 | tf_op jit(solution)/shard_map/ppermute | solution.py:474
  18.3 0.0 collective-permute-done.3.refs_8_
  18.4 1.8 %collective-permute-done.2.refs_7_ = f32[5,8,128]{2,1,0:T(8,128)S(1)} collective-permute-done((f32[5,8,128]{2,1,0:T(8,128)S(1)}, f32[5,8,128]{2,1,0:T(8,128)S(1)}, u32[]{:S(2)}, u32[]{:S(2)}) %collective-permute-start.2) | collective-permute-done | bytes 20512 | tf_op jit(solution)/shard_map/ppermute | solution.py:474
  20.1 5.5 %shard_map.113 = (f32[5,33,16,128]{3,2,1,0:T(8,128)S(1)}, f32[5,16,128]{2,1,0:T(8,128)S(1)}, f32[5,32,128]{2,1,0:T(8,128)S(1)}, f32[5,32,128]{2,1,0:T(8,128)S(1)...) custom-call(f32[5,33,16,128]{3,2,1,0:T(8,128)S(1)} %get-tuple-element.39.refs_0_, ...), custom_call_target="tpu_custom_call" | custom-call | flops 52428800 | bytes 13000704 | tf_op jit(solution)/shard_map/pallas_call | solution.py:33
  25.6 0.0 collective-permute-done.4.refs_5_
  25.6 0.1 shard_map.115
  25.8 0.1 collective-permute-start.5
  25.8 0.1 collective-permute-start.6
  25.9 1.2 %collective-permute-done.5.refs_5_.pair_ref = f32[5,32,128]{2,1,0:T(8,128)S(1)} collective-permute-done((f32[5,32,128]{2,1,0:T(8,128)S(1)}, f32[5,32,128]{2,1,0:T(8,128)S(1)}, u32[]{:S(2)}, u32[]{:S(2)}) %collective-permute-start.5) | collective-permute-done | bytes 81952 | tf_op jit(solution)/shard_map/ppermute | solution.py:471
  27.1 4.8 %collective-permute-done.6.refs_6_.odd_ref = f32[5,32,128]{2,1,0:T(8,128)S(1)} collective-permute-done((f32[5,32,128]{2,1,0:T(8,128)S(1)}, f32[5,32,128]{2,1,0:T(8,128)S(1)}, u32[]{:S(2)}, u32[]{:S(2)}) %collective-permute-start.6) | collective-permute-done | bytes 81952 | tf_op jit(solution)/shard_map/ppermute | solution.py:472
  31.9 0.1 collective-permute-start.9
  32.0 0.1 collective-permute-start.8
  32.1 6.4 %collective-permute-start.7 = (f32[5,8,128]{2,1,0:T(8,128)S(1)}, f32[5,8,128]{2,1,0:T(8,128)S(1)}, u32[]{:S(2)}, u32[]{:S(2)}) collective-permute-start(f32[5,8,128]{2,1,0:T(8,128)S(1)} %get-tuple-element.54), channel_id=1, source_target_pairs={{0,1},{1,0},{2,3},{3,2},{4,5},{5,4},{6,7},{7,6},{8,9},{9,8},{10,11... | collective-permute-start | bytes 61448 | tf_op jit(solution)/shard_map/ppermute | solution.py:474
  38.5 0.0 collective-permute-done.8.refs_8_
  38.5 1.8 %collective-permute-done.7.refs_7_ = f32[5,8,128]{2,1,0:T(8,128)S(1)} collective-permute-done((f32[5,8,128]{2,1,0:T(8,128)S(1)}, f32[5,8,128]{2,1,0:T(8,128)S(1)}, u32[]{:S(2)}, u32[]{:S(2)}) %collective-permute-start.7) | collective-permute-done | bytes 20512 | tf_op jit(solution)/shard_map/ppermute | solution.py:474
  40.3 3.8 %shard_map.116 = (f32[5,33,16,128]{3,2,1,0:T(8,128)S(1)}, f32[5,16,128]{2,1,0:T(8,128)S(1)}, f32[5,32,128]{2,1,0:T(8,128)S(1)}, f32[5,32,128]{2,1,0:T(8,128)S(1)}, f32[5,8,128]{2,1,0:T(8,128)S(1)}) custom-call(f32[5,33,16,128]{3,2,1,0:T(8,128)S(1)} %get-tuple-element.44.refs_0_, f32[5,16,128]{2,1,0:T(8,128)S(1)} %get-tuple-element.50.refs_1_.slab_ref.refs_0_, ...), custom_call_target="tpu_custom_call" | custom-call | flops 52428800 | bytes 22831104 | tf_op jit(solution)/shard_map/pallas_call | solution.py:33
  44.1 0.0 collective-permute-done.9.refs_5_
  44.1 0.1 shard_map.118
  44.3 1.1 %shard_map.119 = (f32[8,8,128]{2,1,0:T(8,128)S(1)}, f32[7,32,128]{2,1,0:T(8,128)S(1)}) custom-call(f32[5,16,128]{2,1,0:T(8,128)S(1)} %get-tuple-element.60.refs_0_.refs_1_.slab_ref, f32[3,5,16,128]{3,2,1,0:T(8,128)S(1)} %copy-done.3, s32[16,128]{1,0:T(8,128)S(1)} %copy-done.2, s32[4,16,128]{2,1,0:T(8,128)S(1)} %copy-done.5, f32[4,16,128]{2,1,0:T(8,128)S(1)} %copy-done.6, ...), custom_call_target="tpu_custom_call" | custom-call | flops 10000000 | bytes 319488 | tf_op jit(solution)/shard_map/pallas_call | solution.py:33
  45.4 0.1 collective-permute-start.10
  45.5 2.7 %collective-permute-start.11 = (f32[5,32,128]{2,1,0:T(8,128)S(1)}, f32[5,32,128]{2,1,0:T(8,128)S(1)}, u32[]{:S(2)}, u32[]{:S(2)}) collective-permute-start(f32[5,32,128]{2,1,0:T(8,128)S(1)} %get-tuple-element.63), channel_id=1, source_target_pairs={{0,120},{8,16},{16,8},{24,32},{32,24},{40,48},{48,40},{56,64},{64,... | collective-permute-start | bytes 245768 | tf_op jit(solution)/shard_map/ppermute | solution.py:472
  48.2 3.4 %collective-permute-done.11.refs_6_.odd_ref = f32[5,32,128]{2,1,0:T(8,128)S(1)} collective-permute-done((f32[5,32,128]{2,1,0:T(8,128)S(1)}, f32[5,32,128]{2,1,0:T(8,128)S(1)}, u32[]{:S(2)}, u32[]{:S(2)}) %collective-permute-start.11) | collective-permute-done | bytes 81952 | tf_op jit(solution)/shard_map/ppermute | solution.py:472
  51.6 0.0 collective-permute-done.10.refs_5_.pair_ref.bundle_ref
  51.6 2.7 %collective-permute-start.14 = (f32[5,24,128]{2,1,0:T(8,128)S(1)}, f32[5,24,128]{2,1,0:T(8,128)S(1)}, u32[]{:S(2)}, u32[]{:S(2)}) collective-permute-start(f32[5,24,128]{2,1,0:T(8,128)S(1)} %shard_map.121), channel_id=1, source_target_pairs={{0,120},{8,112},{16,104},{24,96},{32,88},{40,80},{48,72},{56,64},{... | collective-permute-start | bytes 184328 | tf_op jit(solution)/shard_map/ppermute | solution.py:476
  54.3 0.1 collective-permute-start.15
  54.4 0.1 collective-permute-start.13
  54.5 4.6 %collective-permute-start.12 = (f32[5,8,128]{2,1,0:T(8,128)S(1)}, f32[5,8,128]{2,1,0:T(8,128)S(1)}, u32[]{:S(2)}, u32[]{:S(2)}) collective-permute-start(f32[5,8,128]{2,1,0:T(8,128)S(1)} %get-tuple-element.64), channel_id=1, source_target_pairs={{0,1},{1,0},{2,3},{3,2},{4,5},{5,4},{6,7},{7,6},{8,9},{9,8},{10,11... | collective-permute-start | bytes 61448 | tf_op jit(solution)/shard_map/ppermute | solution.py:474
  59.1 0.0 collective-permute-done.15.got_ref
  59.1 0.1 collective-permute-start.16
  59.2 4.8 %collective-permute-done.16.got_ref = f32[2,8,128]{2,1,0:T(8,128)S(1)} collective-permute-done((f32[2,8,128]{2,1,0:T(8,128)S(1)}, f32[2,8,128]{2,1,0:T(8,128)S(1)}, u32[]{:S(2)}, u32[]{:S(2)}) %collective-permute-start.16) | collective-permute-done | bytes 8224 | tf_op jit(solution)/shard_map/ppermute | solution.py:425
  64.1 1.2 %collective-permute-start.17 = (f32[1,8,128]{2,1,0:T(8,128)S(1)}, f32[1,8,128]{2,1,0:T(8,128)S(1)}, u32[]{:S(2)}, u32[]{:S(2)}) collective-permute-start(f32[1,8,128]{2,1,0:T(8,128)S(1)} %get-tuple-element.74), channel_id=1, source_target_pairs={{0,64},{1,65},{2,66},{3,67},{4,68},{5,69},{6,70},{7,71},{8,72},{9,... | collective-permute-start | bytes 12296 | tf_op jit(solution)/shard_map/ppermute | solution.py:425
  65.3 2.4 %collective-permute-done.17.b_ref = f32[1,8,128]{2,1,0:T(8,128)S(1)} collective-permute-done((f32[1,8,128]{2,1,0:T(8,128)S(1)}, f32[1,8,128]{2,1,0:T(8,128)S(1)}, u32[]{:S(2)}, u32[]{:S(2)}) %collective-permute-start.17) | collective-permute-done | bytes 4128 | tf_op jit(solution)/shard_map/ppermute | solution.py:425
  67.7 1.3 %collective-permute-start.18 = (f32[1,8,128]{2,1,0:T(8,128)S(1)}, f32[1,8,128]{2,1,0:T(8,128)S(1)}, u32[]{:S(2)}, u32[]{:S(2)}) collective-permute-start(f32[1,8,128]{2,1,0:T(8,128)S(1)} %shard_map.126.a_ref), channel_id=1, source_target_pairs={{0,65},{1,64},{2,67},{3,66},{4,69},{5,68},{6,71},{7,70},{8,73},{9,... | collective-permute-start | bytes 12296 | tf_op jit(solution)/shard_map/ppermute | solution.py:425
  69.0 3.5 %collective-permute-done.18.b_ref = f32[1,8,128]{2,1,0:T(8,128)S(1)} collective-permute-done((f32[1,8,128]{2,1,0:T(8,128)S(1)}, f32[1,8,128]{2,1,0:T(8,128)S(1)}, u32[]{:S(2)}, u32[]{:S(2)}) %collective-permute-start.18) | collective-permute-done | bytes 4128 | tf_op jit(solution)/shard_map/ppermute | solution.py:425
  72.5 2.8 %collective-permute-start.21 = (f32[1,8,128]{2,1,0:T(8,128)S(1)}, f32[1,8,128]{2,1,0:T(8,128)S(1)}, u32[]{:S(2)}, u32[]{:S(2)}) collective-permute-start(f32[1,8,128]{2,1,0:T(8,128)S(1)} %shard_map.127.a_ref), channel_id=1, source_target_pairs={{0,4},{1,5},{2,6},{3,7},{4,0},{5,1},{6,2},{7,3},{8,12},{9,13},{10,... | collective-permute-start | bytes 12296 | tf_op jit(solution)/shard_map/ppermute | solution.py:425
  75.3 1.3 %collective-permute-start.20 = (f32[1,8,128]{2,1,0:T(8,128)S(1)}, f32[1,8,128]{2,1,0:T(8,128)S(1)}, u32[]{:S(2)}, u32[]{:S(2)}) collective-permute-start(f32[1,8,128]{2,1,0:T(8,128)S(1)} %shard_map.127.a_ref), channel_id=1, source_target_pairs={{0,6},{1,7},{2,4},{3,5},{4,2},{5,3},{6,0},{7,1},{8,14},{9,15},{10,... | collective-permute-start | bytes 12296 | tf_op jit(solution)/shard_map/ppermute | solution.py:425
  76.7 0.0 collective-permute-done.12.refs_7_
  76.7 4.1 %shard_map.120 = (f32[5,32,16,128]{3,2,1,0:T(8,128)}, f32[5,16,128]{2,1,0:T(8,128)S(1)}, f32[5,32,16,128]{3,2,1,0:T(8,128)}) custom-call(f32[5,33,16,128]{3,2,1,0:T(8,128)S(1)} %get-tuple-element.55.refs_0_, f32[5,16,128]{2,1,0:T(8,128)S(1)} %get-tuple-element.60.refs_0_.refs_1_.slab_ref, f32[3,5,5,32,16,128]{5,4,3,2,1,0:T(8,128)S(1)} %get-tuple-element.51.refs_2_, ...), custom_call_target="tpu_custom_call" | custom-call | flops 52428800 | bytes 22863872 | tf_op jit(solution)/shard_map/pallas_call | solution.py:33
  80.8 0.0 collective-permute-done.21.d_ref
  80.8 0.7 shard_map.128
  81.5 0.7 shard_map.122
  (27 shorter events, 0.2 us)
Async XLA Ops:
  0.6 19.5 %copy-start.1 = (f32[32,16,128]{2,1,0:T(8,128)S(1)}, f32[32,16,128]{2,1,0:T(8,128)}, u32[]{:S(2)}) copy-start(f32[32,16,128]{2,1,0:T(8,128)} %refs_2_.9) | copy-start | bytes 786436
  0.6 19.5 %copy-start = (f32[5,32,16,128]{3,2,1,0:T(8,128)S(1)}, f32[5,32,16,128]{3,2,1,0:T(8,128)}, u32[]{:S(2)}) copy-start(f32[5,32,16,128]{3,2,1,0:T(8,128)} %refs_3_.12) | copy-start | bytes 3932164
  2.4 5.4 %collective-permute-start = (f32[5,32,128]{2,1,0:T(8,128)S(1)}, f32[5,32,128]{2,1,0:T(8,128)S(1)}, u32[]{:S(2)}, u32[]{:S(2)}) collective-permute-start(f32[5,32,128]{2,1,0:T(8,128)S(1)} %get-tuple-element.41), channel_id=1, source_target_pairs={{0,8},{8,0},{16,24},{24,16},{32,40},{40,32},{48,56},{56,48},{64,72... | collective-permute-start | bytes 245768 | tf_op jit(solution)/shard_map/ppermute | solution.py:471
  2.5 7.4 %collective-permute-start.1 = (f32[5,32,128]{2,1,0:T(8,128)S(1)}, f32[5,32,128]{2,1,0:T(8,128)S(1)}, u32[]{:S(2)}, u32[]{:S(2)}) collective-permute-start(f32[5,32,128]{2,1,0:T(8,128)S(1)} %get-tuple-element.42), channel_id=1, source_target_pairs={{0,120},{8,16},{16,8},{24,32},{32,24},{40,48},{48,40},{56,64},{64,... | collective-permute-start | bytes 245768 | tf_op jit(solution)/shard_map/ppermute | solution.py:472
  10.0 15.6 %collective-permute-start.4 = (f32[5,24,128]{2,1,0:T(8,128)S(1)}, f32[5,24,128]{2,1,0:T(8,128)S(1)}, u32[]{:S(2)}, u32[]{:S(2)}) collective-permute-start(f32[5,24,128]{2,1,0:T(8,128)S(1)} %shard_map.114), channel_id=1, source_target_pairs={{0,120},{8,112},{16,104},{24,96},{32,88},{40,80},{48,72},{56,64},{... | collective-permute-start | bytes 184328 | tf_op jit(solution)/shard_map/ppermute | solution.py:476
  13.9 4.5 %collective-permute-start.3 = (f32[5,8,128]{2,1,0:T(8,128)S(1)}, f32[5,8,128]{2,1,0:T(8,128)S(1)}, u32[]{:S(2)}, u32[]{:S(2)}) collective-permute-start(f32[5,8,128]{2,1,0:T(8,128)S(1)} %get-tuple-element.43), channel_id=1, source_target_pairs={{0,8},{1,2},{2,1},{3,4},{4,3},{5,6},{6,5},{7,15},{8,0},{9,10},{10,... | collective-permute-start | bytes 61448 | tf_op jit(solution)/shard_map/ppermute | solution.py:473
  13.9 6.2 %collective-permute-start.2 = (f32[5,8,128]{2,1,0:T(8,128)S(1)}, f32[5,8,128]{2,1,0:T(8,128)S(1)}, u32[]{:S(2)}, u32[]{:S(2)}) collective-permute-start(f32[5,8,128]{2,1,0:T(8,128)S(1)} %get-tuple-element.43), channel_id=1, source_target_pairs={{0,1},{1,0},{2,3},{3,2},{4,5},{5,4},{6,7},{7,6},{8,9},{9,8},{10,11... | collective-permute-start | bytes 61448 | tf_op jit(solution)/shard_map/ppermute | solution.py:474
  20.1 5.5 %copy-start.2 = (s32[16,128]{1,0:T(8,128)S(1)}, s32[16,128]{1,0:T(8,128)}, u32[]{:S(2)}) copy-start(s32[16,128]{1,0:T(8,128)} %refs_3_.13) | copy-start | bytes 24580
  20.1 5.5 %copy-start.4 = (s32[16,128]{1,0:T(8,128)S(1)}, s32[16,128]{1,0:T(8,128)}, u32[]{:S(2)}) copy-start(s32[16,128]{1,0:T(8,128)} %refs_4_.13) | copy-start | bytes 24580
  25.8 1.3 %collective-permute-start.5 = (f32[5,32,128]{2,1,0:T(8,128)S(1)}, f32[5,32,128]{2,1,0:T(8,128)S(1)}, u32[]{:S(2)}, u32[]{:S(2)}) collective-permute-start(f32[5,32,128]{2,1,0:T(8,128)S(1)} %get-tuple-element.52), channel_id=1, source_target_pairs={{0,8},{8,0},{16,24},{24,16},{32,40},{40,32},{48,56},{56,48},{64,72... | collective-permute-start | bytes 245768 | tf_op jit(solution)/shard_map/ppermute | solution.py:471
  25.8 6.1 %collective-permute-start.6 = (f32[5,32,128]{2,1,0:T(8,128)S(1)}, f32[5,32,128]{2,1,0:T(8,128)S(1)}, u32[]{:S(2)}, u32[]{:S(2)}) collective-permute-start(f32[5,32,128]{2,1,0:T(8,128)S(1)} %get-tuple-element.53), channel_id=1, source_target_pairs={{0,120},{8,16},{16,8},{24,32},{32,24},{40,48},{48,40},{56,64},{64,... | collective-permute-start | bytes 245768 | tf_op jit(solution)/shard_map/ppermute | solution.py:472
  31.9 12.2 %collective-permute-start.9 = (f32[5,24,128]{2,1,0:T(8,128)S(1)}, f32[5,24,128]{2,1,0:T(8,128)S(1)}, u32[]{:S(2)}, u32[]{:S(2)}) collective-permute-start(f32[5,24,128]{2,1,0:T(8,128)S(1)} %shard_map.117), channel_id=1, source_target_pairs={{0,120},{8,112},{16,104},{24,96},{32,88},{40,80},{48,72},{56,64},{... | collective-permute-start | bytes 184328 | tf_op jit(solution)/shard_map/ppermute | solution.py:476
  32.0 6.5 %collective-permute-start.8 = (f32[5,8,128]{2,1,0:T(8,128)S(1)}, f32[5,8,128]{2,1,0:T(8,128)S(1)}, u32[]{:S(2)}, u32[]{:S(2)}) collective-permute-start(f32[5,8,128]{2,1,0:T(8,128)S(1)} %get-tuple-element.54), channel_id=1, source_target_pairs={{0,8},{1,2},{2,1},{3,4},{4,3},{5,6},{6,5},{7,15},{8,0},{9,10},{10,... | collective-permute-start | bytes 61448 | tf_op jit(solution)/shard_map/ppermute | solution.py:473
  32.1 8.1 %collective-permute-start.7 = (f32[5,8,128]{2,1,0:T(8,128)S(1)}, f32[5,8,128]{2,1,0:T(8,128)S(1)}, u32[]{:S(2)}, u32[]{:S(2)}) collective-permute-start(f32[5,8,128]{2,1,0:T(8,128)S(1)} %get-tuple-element.54), channel_id=1, source_target_pairs={{0,1},{1,0},{2,3},{3,2},{4,5},{5,4},{6,7},{7,6},{8,9},{9,8},{10,11... | collective-permute-start | bytes 61448 | tf_op jit(solution)/shard_map/ppermute | solution.py:474
  40.3 4.0 %copy-start.3 = (f32[3,5,16,128]{3,2,1,0:T(8,128)S(1)}, f32[3,5,16,128]{3,2,1,0:T(8,128)}, u32[]{:S(2)}) copy-start(f32[3,5,16,128]{3,2,1,0:T(8,128)} %refs_1_.1) | copy-start | bytes 368644
  40.3 4.0 %copy-start.5 = (s32[4,16,128]{2,1,0:T(8,128)S(1)}, s32[4,16,128]{2,1,0:T(8,128)}, u32[]{:S(2)}) copy-start(s32[4,16,128]{2,1,0:T(8,128)} %refs_3_.11) | copy-start | bytes 98308
  40.3 4.0 %copy-start.6 = (f32[4,16,128]{2,1,0:T(8,128)S(1)}, f32[4,16,128]{2,1,0:T(8,128)}, u32[]{:S(2)}) copy-start(f32[4,16,128]{2,1,0:T(8,128)} %refs_4_.11) | copy-start | bytes 98308
  45.4 6.2 %collective-permute-start.10 = (f32[7,32,128]{2,1,0:T(8,128)S(1)}, f32[7,32,128]{2,1,0:T(8,128)S(1)}, u32[]{:S(2)}, u32[]{:S(2)}) collective-permute-start(f32[7,32,128]{2,1,0:T(8,128)S(1)} %get-tuple-element.62), channel_id=1, source_target_pairs={{0,8},{8,0},{16,24},{24,16},{32,40},{40,32},{48,56},{56,48},{64,72... | collective-permute-start | bytes 344072 | tf_op jit(solution)/shard_map/ppermute | solution.py:471
  45.5 6.1 %collective-permute-start.11 = (f32[5,32,128]{2,1,0:T(8,128)S(1)}, f32[5,32,128]{2,1,0:T(8,128)S(1)}, u32[]{:S(2)}, u32[]{:S(2)}) collective-permute-start(f32[5,32,128]{2,1,0:T(8,128)S(1)} %get-tuple-element.63), channel_id=1, source_target_pairs={{0,120},{8,16},{16,8},{24,32},{32,24},{40,48},{48,40},{56,64},{64,... | collective-permute-start | bytes 245768 | tf_op jit(solution)/shard_map/ppermute | solution.py:472
  51.6 29.9 %collective-permute-start.14 = (f32[5,24,128]{2,1,0:T(8,128)S(1)}, f32[5,24,128]{2,1,0:T(8,128)S(1)}, u32[]{:S(2)}, u32[]{:S(2)}) collective-permute-start(f32[5,24,128]{2,1,0:T(8,128)S(1)} %shard_map.121), channel_id=1, source_target_pairs={{0,120},{8,112},{16,104},{24,96},{32,88},{40,80},{48,72},{56,64},{... | collective-permute-start | bytes 184328 | tf_op jit(solution)/shard_map/ppermute | solution.py:476
  54.3 4.8 %collective-permute-start.15 = (f32[4,8,128]{2,1,0:T(8,128)S(1)}, f32[4,8,128]{2,1,0:T(8,128)S(1)}, u32[]{:S(2)}, u32[]{:S(2)}) collective-permute-start(f32[4,8,128]{2,1,0:T(8,128)S(1)} %get-tuple-element.70), channel_id=1, source_target_pairs={{0,16},{1,17},{2,18},{3,19},{4,20},{5,21},{6,22},{7,23},{8,24},{9,... | collective-permute-start | bytes 49160 | tf_op jit(solution)/shard_map/ppermute | solution.py:425
  54.4 22.3 %collective-permute-start.13 = (f32[5,8,128]{2,1,0:T(8,128)S(1)}, f32[5,8,128]{2,1,0:T(8,128)S(1)}, u32[]{:S(2)}, u32[]{:S(2)}) collective-permute-start(f32[5,8,128]{2,1,0:T(8,128)S(1)} %get-tuple-element.64), channel_id=1, source_target_pairs={{0,8},{1,2},{2,1},{3,4},{4,3},{5,6},{6,5},{7,15},{8,0},{9,10},{10,... | collective-permute-start | bytes 61448 | tf_op jit(solution)/shard_map/ppermute | solution.py:473
  54.5 22.2 %collective-permute-start.12 = (f32[5,8,128]{2,1,0:T(8,128)S(1)}, f32[5,8,128]{2,1,0:T(8,128)S(1)}, u32[]{:S(2)}, u32[]{:S(2)}) collective-permute-start(f32[5,8,128]{2,1,0:T(8,128)S(1)} %get-tuple-element.64), channel_id=1, source_target_pairs={{0,1},{1,0},{2,3},{3,2},{4,5},{5,4},{6,7},{7,6},{8,9},{9,8},{10,11... | collective-permute-start | bytes 61448 | tf_op jit(solution)/shard_map/ppermute | solution.py:474
  59.1 4.9 %collective-permute-start.16 = (f32[2,8,128]{2,1,0:T(8,128)S(1)}, f32[2,8,128]{2,1,0:T(8,128)S(1)}, u32[]{:S(2)}, u32[]{:S(2)}) collective-permute-start(f32[2,8,128]{2,1,0:T(8,128)S(1)} %get-tuple-element.72), channel_id=1, source_target_pairs={{0,48},{1,49},{2,50},{3,51},{4,52},{5,53},{6,54},{7,55},{8,56},{9,... | collective-permute-start | bytes 24584 | tf_op jit(solution)/shard_map/ppermute | solution.py:425
  64.1 3.6 %collective-permute-start.17 = (f32[1,8,128]{2,1,0:T(8,128)S(1)}, f32[1,8,128]{2,1,0:T(8,128)S(1)}, u32[]{:S(2)}, u32[]{:S(2)}) collective-permute-start(f32[1,8,128]{2,1,0:T(8,128)S(1)} %get-tuple-element.74), channel_id=1, source_target_pairs={{0,64},{1,65},{2,66},{3,67},{4,68},{5,69},{6,70},{7,71},{8,72},{9,... | collective-permute-start | bytes 12296 | tf_op jit(solution)/shard_map/ppermute | solution.py:425
  67.7 4.8 %collective-permute-start.18 = (f32[1,8,128]{2,1,0:T(8,128)S(1)}, f32[1,8,128]{2,1,0:T(8,128)S(1)}, u32[]{:S(2)}, u32[]{:S(2)}) collective-permute-start(f32[1,8,128]{2,1,0:T(8,128)S(1)} %shard_map.126.a_ref), channel_id=1, source_target_pairs={{0,65},{1,64},{2,67},{3,66},{4,69},{5,68},{6,71},{7,70},{8,73},{9,... | collective-permute-start | bytes 12296 | tf_op jit(solution)/shard_map/ppermute | solution.py:425
  72.5 8.2 %collective-permute-start.21 = (f32[1,8,128]{2,1,0:T(8,128)S(1)}, f32[1,8,128]{2,1,0:T(8,128)S(1)}, u32[]{:S(2)}, u32[]{:S(2)}) collective-permute-start(f32[1,8,128]{2,1,0:T(8,128)S(1)} %shard_map.127.a_ref), channel_id=1, source_target_pairs={{0,4},{1,5},{2,6},{3,7},{4,0},{5,1},{6,2},{7,3},{8,12},{9,13},{10,... | collective-permute-start | bytes 12296 | tf_op jit(solution)/shard_map/ppermute | solution.py:425
  75.3 5.4 %collective-permute-start.20 = (f32[1,8,128]{2,1,0:T(8,128)S(1)}, f32[1,8,128]{2,1,0:T(8,128)S(1)}, u32[]{:S(2)}, u32[]{:S(2)}) collective-permute-start(f32[1,8,128]{2,1,0:T(8,128)S(1)} %shard_map.127.a_ref), channel_id=1, source_target_pairs={{0,6},{1,7},{2,4},{3,5},{4,2},{5,3},{6,0},{7,1},{8,14},{9,15},{10,... | collective-permute-start | bytes 12296 | tf_op jit(solution)/shard_map/ppermute | solution.py:425
  76.7 4.1 %collective-permute-start.19 = (f32[1,8,128]{2,1,0:T(8,128)S(1)}, f32[1,8,128]{2,1,0:T(8,128)S(1)}, u32[]{:S(2)}, u32[]{:S(2)}) collective-permute-start(f32[1,8,128]{2,1,0:T(8,128)S(1)} %shard_map.127.a_ref), channel_id=1, source_target_pairs={{0,2},{1,3},{2,0},{3,1},{4,6},{5,7},{6,4},{7,5},{8,10},{9,11},{10,... | collective-permute-start | bytes 12296 | tf_op jit(solution)/shard_map/ppermute | solution.py:425
